TPU v7x, 512 devices: a whole 4x4x16 slice. The times are simulated.
512 devices in a mesh: row: 128 (over x, z, core), mp: 4 (over y).
Axes of the slice: x: 4, y: 4, z: 16, core: 2. Of those that a mesh axis runs over, the one named last changes fastest.
Arguments:
- queries: bfloat16 [768, 16384], P('mp', 'row'), may hold values from -36 to 36
- key_cells: bfloat16 [768, 16384], P('mp', 'row'), may hold values from -7 to 7
- value_cells: bfloat16 [768, 16384], P('mp', 'row'), may hold values from -6 to 6
- out_weight: bfloat16 [768, 768], P('mp'), may hold values from -0.21875 to 0.21875
- out_cotangent: bfloat16 [768, 16384], P('mp', 'row'), may hold values from -6 to 6
- parent_rows: int32 [128, 64], P('row'), may hold values from 0 to 1023, as said below
- window_reach: int32 [128], P('row'), may hold values from 0 to 1
- valid_cells: int32 [128], P('row'), may hold values from 64 to 128, as said below
Outputs:
- mixed: bfloat16 [768, 16384], P('mp', 'row')
- d_queries: bfloat16 [768, 16384], P('mp', 'row')
- d_key_cells: bfloat16 [768, 16384], P('mp', 'row')
- d_value_cells: bfloat16 [768, 16384], P('mp', 'row')
- weight_grad: float32 [768, 768], P('mp')
Inputs may be any that keep to these rules, and one draw needn't show every extreme that they name: `parent_rows`: the rows named by the blocks of one device (the 1 block in a row of the array that share an index of row) lie on pairwise different devices, where a device holds 8 consecutive rows; every named row lies wholly below its block's valid_cells. `valid_cells`: A multiple of 16.
All inputs are finite; a program needn't handle non-finite values.
Results may differ from a plain program's by a relative error of at most 0.012.
Values may be sent and summed in bfloat16 or wider, within the bound.
A program may use at most 64 MiB of HBM per device.

v0:
```python
import jax
import jax.numpy as jnp
from jax import lax
from jax.sharding import PartitionSpec as P

HEAD_DIM = 64
CELLS_BLK = 128
ROW_CELLS = 16
ROWS_BLK = 8


def shifted(block, axis, distance):
    devices = range(lax.axis_size(axis))
    route = [(i - distance, i) for i in devices if i - distance in devices]
    return lax.ppermute(block, axis, route)


def masked_softmax(scores, visible):
    masked = jnp.where(visible, scores, -1e30)
    top_score = jnp.max(masked, axis=-1, keepdims=True)
    exponent = jnp.exp(jnp.where(visible, scores - top_score, -1e30))
    return exponent / jnp.sum(exponent, axis=-1, keepdims=True)


def on_device(
    queries,
    key_cells,
    value_cells,
    out_weight,
    out_cotangent,
    parent_rows,
    window_reach,
    valid_cells,
):
    query_rows = queries.T
    key_rows_in = key_cells.T
    value_rows_in = value_cells.T
    nblocks = valid_cells.shape[0]
    fanout = parent_rows.shape[1]
    feature_width = query_rows.shape[1]
    heads_here = feature_width // HEAD_DIM
    cell_count = nblocks * CELLS_BLK
    n_row = lax.axis_size("row")
    device_index = lax.axis_index("row")
    rows_dev = nblocks * ROWS_BLK
    score_scale = HEAD_DIM ** (-0.5)
    query_blocks = query_rows.reshape(nblocks, CELLS_BLK, heads_here, HEAD_DIM)
    key_blocks = key_rows_in.reshape(nblocks, CELLS_BLK, feature_width)
    value_blocks = value_rows_in.reshape(nblocks, CELLS_BLK, feature_width)
    cell_ids = jnp.arange(CELLS_BLK)
    own_ok = cell_ids[None, :] < valid_cells[:, None]
    last_mask = own_ok[-1].astype(jnp.bfloat16)
    edge_keys, edge_values, edge_mask = shifted(
        (key_blocks[-1], value_blocks[-1], last_mask), "row", 1
    )
    prior_keys = jnp.concatenate([edge_keys[None], key_blocks[:-1]], axis=0)
    prior_values = jnp.concatenate([edge_values[None], value_blocks[:-1]], axis=0)
    prior_valid = jnp.concatenate([(edge_mask > 0.5)[None], own_ok[:-1]], axis=0)
    block_ids = device_index * nblocks + jnp.arange(nblocks)
    prior_ok = prior_valid & (window_reach[:, None] == 1) & (block_ids[:, None] > 0)
    wanted = parent_rows.reshape(-1)
    owners = wanted // rows_dev
    local_rows = wanted - owners * rows_dev
    onehot = owners[:, None] == jnp.arange(n_row)[None, :]
    asking = jnp.sum(jnp.where(onehot, local_rows[:, None], 0), axis=0)
    asked_rows = lax.all_to_all(
        asking.reshape(n_row, 1), "row", split_axis=0, concat_axis=0, tiled=True
    ).reshape(n_row)
    key_table = key_rows_in.reshape(rows_dev, ROW_CELLS * feature_width)
    value_table = value_rows_in.reshape(rows_dev, ROW_CELLS * feature_width)
    fetched_keys, fetched_values = (
        lax.all_to_all(
            jnp.take(key_table, asked_rows, axis=0), "row", split_axis=0, concat_axis=0, tiled=True
        ),
        lax.all_to_all(
            jnp.take(value_table, asked_rows, axis=0),
            "row",
            split_axis=0,
            concat_axis=0,
            tiled=True,
        ),
    )
    parent_keys = jnp.take(fetched_keys, owners, axis=0).reshape(
        nblocks, fanout * ROW_CELLS, feature_width
    )
    parent_values = jnp.take(fetched_values, owners, axis=0).reshape(
        nblocks, fanout * ROW_CELLS, feature_width
    )
    block_keys = jnp.concatenate([prior_keys, key_blocks, parent_keys], axis=1).reshape(
        nblocks, -1, heads_here, HEAD_DIM
    )
    block_values = jnp.concatenate([prior_values, value_blocks, parent_values], axis=1).reshape(
        nblocks, -1, heads_here, HEAD_DIM
    )
    key_mask = jnp.concatenate(
        [prior_ok, own_ok, jnp.ones((nblocks, fanout * ROW_CELLS), bool)], axis=1
    )
    scores = (
        jnp.einsum("bqhd,bkhd->bhqk", query_blocks, block_keys, preferred_element_type=jnp.float32)
        * score_scale
    )
    prob_full = masked_softmax(scores, key_mask[:, None, None, :])
    probs_low = prob_full.astype(jnp.bfloat16)
    attended = jnp.einsum(
        "bhqk,bkhd->bqhd", probs_low, block_values, preferred_element_type=jnp.float32
    )
    attended = attended.astype(jnp.bfloat16).reshape(cell_count, feature_width)
    partial_out = lax.dot_general(
        out_weight, attended, (((0,), (1,)), ((), ())), preferred_element_type=jnp.float32
    )
    mixed = lax.psum_scatter(
        partial_out.astype(jnp.bfloat16), "mp", scatter_dimension=0, tiled=True
    )
    cotangent_all = lax.all_gather(out_cotangent, "mp", axis=0, tiled=True)
    d_attended = lax.dot_general(
        cotangent_all, out_weight, (((0,), (1,)), ((), ())), preferred_element_type=jnp.float32
    ).astype(jnp.bfloat16)
    weight_part = lax.dot_general(
        attended, cotangent_all, (((0,), (1,)), ((), ())), preferred_element_type=jnp.float32
    )
    weight_grad = lax.psum(weight_part, "row")
    d_heads = d_attended.reshape(nblocks, CELLS_BLK, heads_here, HEAD_DIM)
    d_probs = jnp.einsum(
        "bqhd,bkhd->bhqk", d_heads, block_values, preferred_element_type=jnp.float32
    )
    row_delta = jnp.sum(prob_full * d_probs, axis=-1, keepdims=True)
    d_scores = (prob_full * (d_probs - row_delta) * score_scale).astype(jnp.bfloat16)
    d_queries = jnp.einsum(
        "bhqk,bkhd->bqhd", d_scores, block_keys, preferred_element_type=jnp.float32
    )
    d_queries = d_queries.astype(jnp.bfloat16).reshape(cell_count, feature_width)
    d_keys = jnp.einsum(
        "bhqk,bqhd->bkhd", d_scores, query_blocks, preferred_element_type=jnp.float32
    ).reshape(nblocks, -1, feature_width)
    d_values = jnp.einsum(
        "bhqk,bqhd->bkhd", probs_low, d_heads, preferred_element_type=jnp.float32
    ).reshape(nblocks, -1, feature_width)
    return_keys, return_values = (
        shifted(d_keys[0, :CELLS_BLK].astype(jnp.bfloat16), "row", -1).astype(jnp.float32),
        shifted(d_values[0, :CELLS_BLK].astype(jnp.bfloat16), "row", -1).astype(jnp.float32),
    )
    key_total = (
        d_keys[:, CELLS_BLK : 2 * CELLS_BLK]
        .at[:-1]
        .add(d_keys[1:, :CELLS_BLK])
        .at[-1]
        .add(return_keys)
    )
    value_total = (
        d_values[:, CELLS_BLK : 2 * CELLS_BLK]
        .at[:-1]
        .add(d_values[1:, :CELLS_BLK])
        .at[-1]
        .add(return_values)
    )
    slot_shape = (n_row, ROW_CELLS * feature_width)
    slot_keys = (
        jnp.zeros(slot_shape, jnp.float32)
        .at[owners]
        .add(d_keys[:, 2 * CELLS_BLK :].reshape(nblocks * fanout, ROW_CELLS * feature_width))
    )
    slot_values = (
        jnp.zeros(slot_shape, jnp.float32)
        .at[owners]
        .add(d_values[:, 2 * CELLS_BLK :].reshape(nblocks * fanout, ROW_CELLS * feature_width))
    )
    owner_keys, owner_values = (
        lax.all_to_all(
            slot_keys.astype(jnp.bfloat16), "row", split_axis=0, concat_axis=0, tiled=True
        ).astype(slot_keys.dtype),
        lax.all_to_all(
            slot_values.astype(jnp.bfloat16), "row", split_axis=0, concat_axis=0, tiled=True
        ).astype(slot_values.dtype),
    )
    key_rows = key_total.reshape(rows_dev, ROW_CELLS * feature_width).at[asked_rows].add(owner_keys)
    value_rows = (
        value_total.reshape(rows_dev, ROW_CELLS * feature_width).at[asked_rows].add(owner_values)
    )
    d_key_cells = key_rows.reshape(cell_count, feature_width).astype(jnp.bfloat16)
    d_value_cells = value_rows.reshape(cell_count, feature_width).astype(jnp.bfloat16)
    return (mixed, d_queries.T, d_key_cells.T, d_value_cells.T, weight_grad)


def solution(mesh):
    return jax.shard_map(
        on_device,
        mesh=mesh,
        in_specs=(
            P("mp", "row"),
            P("mp", "row"),
            P("mp", "row"),
            P("mp", None),
            P("mp", "row"),
            P("row", None),
            P("row"),
            P("row"),
        ),
        out_specs=(P("mp", "row"), P("mp", "row"), P("mp", "row"), P("mp", "row"), P("mp", None)),
        check_vma=False,
    )
```

profile of v0, /device:TPU:1, one launch (start us, length us, event | category | flops | bytes accessed | tf_op | source)
XLA Modules:
  0.0 596.7 jit_solution(892980042873338852)
XLA Ops:
  10.2 20.4 %all-to-all-start = ((s32[128,1,1]{2,1,0:T(1,128)}), s32[128,1,1]{2,1,0:T(1,128)S(1)}, u32[]{:S(2)}, u32[]{:S(2)}) async-start(s32[128,1,1]{2,1,0:T(1,128)} %copy.122), calls=%async_computation | async-start | bytes 131072 | tf_op jit(solution)/shard_map/all_to_all | solution.py:66
  32.7 12.9 %all-to-all-done = s32[128,1,1]{2,1,0:T(1,128)S(1)} async-done(((s32[128,1,1]{2,1,0:T(1,128)}), s32[128,1,1]{2,1,0:T(1,128)S(1)}, u32[]{:S(2)}, u32[]{:S(2)}) %all-to-all-start) | async-done | bytes 544 | tf_op jit(solution)/shard_map/all_to_all | solution.py:66
  45.6 2.3 reduce.11
  48.0 1.0 gather_fusion.2
  49.0 1.0 gather_fusion
  50.1 1.1 select_bitcast_fusion
  51.7 1.2 reduce.15
  52.9 1.5 reshape.509
  54.4 6.6 %all-to-all-start.2 = ((bf16[128,2,1536]{2,1,0:T(2,128)(2,1)}), bf16[128,2,1536]{2,1,0:T(2,128)(2,1)S(1)}, u32[]{:S(2)}, u32[]{:S(2)}) async-start(bf16[128,2,1536]{2,1,0:T(2,128)(2,1)} %reshape.509), calls=%async_computation.2 | async-start | bytes 1572864 | tf_op jit(solution)/shard_map/all_to_all | solution.py:72
  60.9 1.2 reduce.16
  62.2 1.4 reshape.507
  63.6 40.9 %all-to-all-done.2 = bf16[128,2,1536]{2,1,0:T(2,128)(2,1)S(1)} async-done(((bf16[128,2,1536]{2,1,0:T(2,128)(2,1)}), bf16[128,2,1536]{2,1,0:T(2,128)(2,1)S(1)}, u32[]{:S(2)}, u32[]{:S(2)}) %all-to-all-start.2) | async-done | bytes 786464 | tf_op jit(solution)/shard_map/all_to_all | solution.py:72
  104.5 8.5 %all-to-all-start.1 = ((bf16[128,2,1536]{2,1,0:T(2,128)(2,1)}), bf16[128,2,1536]{2,1,0:T(2,128)(2,1)}, u32[]{:S(2)}, u32[]{:S(2)}) async-start(bf16[128,2,1536]{2,1,0:T(2,128)(2,1)} %reshape.507), calls=%async_computation.1 | async-start | bytes 1572864 | tf_op jit(solution)/shard_map/all_to_all | solution.py:75
  113.0 3.5 collective-permute-start
  116.6 2.1 collective-permute-start.2
  119.3 3.3 collective-permute-start.1
  123.3 11.4 %all_gather.3 = bf16[768,128]{1,0:T(8,128)(2,1)S(1)} all-gather(bf16[192,128]{1,0:T(8,128)(2,1)S(1)} %copy-done.10), channel_id=1, replica_groups=mesh['row'=128,'mp'=4] {'mp'}, dimensions={0}, use_global_device_ids=true | all-gather | bytes 245760 | tf_op jit(solution)/shard_map/all_gather | solution.py:114
  136.2 8.1 %collective-permute-done.1 = bf16[128]{0:T(256)(128)(2,1)S(1)} collective-permute-done((bf16[128]{0:T(256)(128)(2,1)S(1)}, bf16[128]{0:T(256)(128)(2,1)S(1)}, u32[]{:S(2)}, u32[]{:S(2)}) %collective-permute-start.1) | collective-permute-done | bytes 288 | tf_op jit(solution)/shard_map/ppermute | solution.py:15
  145.2 11.0 %all-to-all-done.1 = bf16[128,2,1536]{2,1,0:T(2,128)(2,1)} async-done(((bf16[128,2,1536]{2,1,0:T(2,128)(2,1)}), bf16[128,2,1536]{2,1,0:T(2,128)(2,1)}, u32[]{:S(2)}, u32[]{:S(2)}) %all-to-all-start.1) | async-done | bytes 786464 | tf_op jit(solution)/shard_map/all_to_all | solution.py:75
  156.2 5.0 reshape.508
  164.8 1.3 convolution_multiply_fusion
  166.1 1.9 fusion.65
  169.4 2.6 fusion.42
  172.0 4.1 fusion.13
  176.1 1.0 copy-done.4
  177.9 2.1 scatter_custom_fusion
  180.1 1.2 reduce.17
  181.3 1.5 reshape.511
  182.8 9.7 %all-to-all-start.3 = ((bf16[128,2,1536]{2,1,0:T(2,128)(2,1)}), bf16[128,2,1536]{2,1,0:T(2,128)(2,1)}, u32[]{:S(2)}, u32[]{:S(2)}) async-start(bf16[128,2,1536]{2,1,0:T(2,128)(2,1)} %reshape.511), calls=%async_computation.3 | async-start | bytes 1572864 | tf_op jit(solution)/shard_map/all_to_all | solution.py:168
  192.5 2.0 fusion.48
  194.5 1.0 copy-done.5
  196.4 2.1 scatter_custom_fusion.2
  198.6 1.2 reduce.18
  199.8 1.5 reshape.513
  201.2 34.5 %all-to-all-done.3 = bf16[128,2,1536]{2,1,0:T(2,128)(2,1)} async-done(((bf16[128,2,1536]{2,1,0:T(2,128)(2,1)}), bf16[128,2,1536]{2,1,0:T(2,128)(2,1)}, u32[]{:S(2)}, u32[]{:S(2)}) %all-to-all-start.3) | async-done | bytes 786464 | tf_op jit(solution)/shard_map/all_to_all | solution.py:168
  235.7 8.1 %all-to-all-start.4 = ((bf16[128,2,1536]{2,1,0:T(2,128)(2,1)}), bf16[128,2,1536]{2,1,0:T(2,128)(2,1)S(1)}, u32[]{:S(2)}, u32[]{:S(2)}) async-start(bf16[128,2,1536]{2,1,0:T(2,128)(2,1)} %reshape.513), calls=%async_computation.4 | async-start | bytes 1572864 | tf_op jit(solution)/shard_map/all_to_all | solution.py:171
  245.3 1.9 convolution_convert_fusion.1
  247.3 1.1 fusion.66
  250.4 2.8 collective-permute-start.3
  253.2 4.8 fusion.23
  258.8 1.9 collective-permute-start.4
  260.7 18.4 %collective-permute-done.3 = bf16[128,192]{0,1:T(8,128)(2,1)S(1)} collective-permute-done((bf16[128,192]{0,1:T(8,128)(2,1)S(1)}, bf16[128,192]{0,1:T(8,128)(2,1)S(1)}, u32[]{:S(2)}, u32[]{:S(2)}) %collective-permute-start.3) | collective-permute-done | bytes 49184 | tf_op jit(solution)/shard_map/ppermute | solution.py:15
  280.3 0.9 slice_add_fusion
  281.4 5.1 reshape.512
  286.5 3.0 scatter_custom_fusion.1
  291.0 3.3 scatter_custom_fusion.3
  295.1 292.2 %all-reduce.2.cloned.1.call-done = f32[192,768]{1,0:T(8,128)} async-done(((f32[192,768]{1,0:T(8,128)}), f32[192,768]{1,0:T(8,128)}) %all-reduce.2.cloned.1.call-update) | async-done | bytes 589840 | tf_op jit(solution)/shard_map/psum | solution.py:121
  587.3 1.9 copy.177
  (91 shorter events, 22.0 us)
Async XLA Ops:
  8.0 127.3 %copy-start = (bf16[192,768]{1,0:T(8,128)(2,1)S(1)}, bf16[192,768]{1,0:T(8,128)(2,1)}, u32[]{:S(2)}) copy-start(bf16[192,768]{1,0:T(8,128)(2,1)} %param.19) | copy-start | bytes 884740
  10.2 35.4 %all-to-all-start = ((s32[128,1,1]{2,1,0:T(1,128)}), s32[128,1,1]{2,1,0:T(1,128)S(1)}, u32[]{:S(2)}, u32[]{:S(2)}) async-start(s32[128,1,1]{2,1,0:T(1,128)} %copy.122), calls=%async_computation | async-start | bytes 131072 | tf_op jit(solution)/shard_map/all_to_all | solution.py:66
  52.9 8.1 %copy-start.1 = (bf16[128,1,3072]{2,0,1:T(8,128)(2,1)S(1)}, bf16[128,1,3072]{2,0,1:T(8,128)(2,1)}, u32[]{:S(2)}) copy-start(bf16[128,1,3072]{2,0,1:T(8,128)(2,1)} %get-tuple-element.66) | copy-start | bytes 2359300
  54.4 50.2 %all-to-all-start.2 = ((bf16[128,2,1536]{2,1,0:T(2,128)(2,1)}), bf16[128,2,1536]{2,1,0:T(2,128)(2,1)S(1)}, u32[]{:S(2)}, u32[]{:S(2)}) async-start(bf16[128,2,1536]{2,1,0:T(2,128)(2,1)} %reshape.509), calls=%async_computation.2 | async-start | bytes 1572864 | tf_op jit(solution)/shard_map/all_to_all | solution.py:72
  62.1 50.9 %copy-start.6 = (bf16[192,128]{1,0:T(8,128)(2,1)S(1)}, bf16[192,128]{1,0:T(8,128)(2,1)}, u32[]{:S(2)}) copy-start(bf16[192,128]{1,0:T(8,128)(2,1)} %param.18) | copy-start | bytes 147460
  62.1 54.4 %copy-start.7 = (bf16[192,128]{1,0:T(8,128)(2,1)S(1)}, bf16[192,128]{1,0:T(8,128)(2,1)}, u32[]{:S(2)}) copy-start(bf16[192,128]{1,0:T(8,128)(2,1)} %param.17) | copy-start | bytes 147460
  62.1 61.2 %copy-start.10 = (bf16[192,128]{1,0:T(8,128)(2,1)S(1)}, bf16[192,128]{1,0:T(8,128)(2,1)}, u32[]{:S(2)}) copy-start(bf16[192,128]{1,0:T(8,128)(2,1)} %param.20) | copy-start | bytes 147460
  62.2 72.6 %copy-start.12 = (s32[1,64]{1,0:T(1,128)S(1)}, s32[1,64]{1,0:T(1,128)}, u32[]{:S(2)}) copy-start(s32[1,64]{1,0:T(1,128)} %param.21) | copy-start | bytes 772
  104.5 51.7 %all-to-all-start.1 = ((bf16[128,2,1536]{2,1,0:T(2,128)(2,1)}), bf16[128,2,1536]{2,1,0:T(2,128)(2,1)}, u32[]{:S(2)}, u32[]{:S(2)}) async-start(bf16[128,2,1536]{2,1,0:T(2,128)(2,1)} %reshape.507), calls=%async_computation.1 | async-start | bytes 1572864 | tf_op jit(solution)/shard_map/all_to_all | solution.py:75
  113.0 56.4 %collective-permute-start = (bf16[128,192]{0,1:T(8,128)(2,1)S(1)}, bf16[128,192]{0,1:T(8,128)(2,1)}, u32[]{:S(2)}, u32[]{:S(2)}) collective-permute-start(bf16[128,192]{0,1:T(8,128)(2,1)S(1)} %bitcast.145), channel_id=1, source_target_pairs={{0,4},{4,8},{8,12},{12,16},{16,20},{20,24},{24,28},{28,32},{32,36}... | collective-permute-start | bytes 147464 | tf_op jit(solution)/shard_map/ppermute | solution.py:15
  116.6 48.1 %collective-permute-start.2 = (bf16[128,192]{0,1:T(8,128)(2,1)S(1)}, bf16[128,192]{0,1:T(8,128)(2,1)}, u32[]{:S(2)}, u32[]{:S(2)}) collective-permute-start(bf16[128,192]{0,1:T(8,128)(2,1)S(1)} %bitcast.149), channel_id=1, source_target_pairs={{0,4},{4,8},{8,12},{12,16},{16,20},{20,24},{24,28},{28,32},{32,36}... | collective-permute-start | bytes 147464 | tf_op jit(solution)/shard_map/ppermute | solution.py:15
  119.3 24.9 %collective-permute-start.1 = (bf16[128]{0:T(256)(128)(2,1)S(1)}, bf16[128]{0:T(256)(128)(2,1)S(1)}, u32[]{:S(2)}, u32[]{:S(2)}) collective-permute-start(bf16[128]{0:T(256)(128)(2,1)S(1)} %compare_convert_fusion), channel_id=1, source_target_pairs={{0,4},{4,8},{8,12},{12,16},{16,20},{20,24},{24,28},{28,32},{32,36}... | collective-permute-start | bytes 776 | tf_op jit(solution)/shard_map/ppermute | solution.py:15
  134.7 9.6 %copy-start.2 = (bf16[768,128]{1,0:T(8,128)(2,1)}, bf16[768,128]{1,0:T(8,128)(2,1)S(1)}, u32[]{:S(2)}) copy-start(bf16[768,128]{1,0:T(8,128)(2,1)S(1)} %all_gather.3) | copy-start | bytes 589828
  163.1 1.6 copy-start.11
  167.9 1.5 copy-start.8
  176.1 1.0 copy-start.4
  181.3 11.2 %copy-start.9 = (bf16[128,192]{0,1:T(8,128)(2,1)S(1)}, bf16[128,192]{0,1:T(8,128)(2,1)}, u32[]{:S(2)}) copy-start(bf16[128,192]{0,1:T(8,128)(2,1)} %convolution_convert_fusion.2) | copy-start | bytes 147460
  182.8 52.9 %all-to-all-start.3 = ((bf16[128,2,1536]{2,1,0:T(2,128)(2,1)}), bf16[128,2,1536]{2,1,0:T(2,128)(2,1)}, u32[]{:S(2)}, u32[]{:S(2)}) async-start(bf16[128,2,1536]{2,1,0:T(2,128)(2,1)} %reshape.511), calls=%async_computation.3 | async-start | bytes 1572864 | tf_op jit(solution)/shard_map/all_to_all | solution.py:168
  194.5 1.0 copy-start.5
  235.7 54.7 %all-to-all-start.4 = ((bf16[128,2,1536]{2,1,0:T(2,128)(2,1)}), bf16[128,2,1536]{2,1,0:T(2,128)(2,1)S(1)}, u32[]{:S(2)}, u32[]{:S(2)}) async-start(bf16[128,2,1536]{2,1,0:T(2,128)(2,1)} %reshape.513), calls=%async_computation.4 | async-start | bytes 1572864 | tf_op jit(solution)/shard_map/all_to_all | solution.py:171
  243.8 343.5 %all-reduce.2.cloned.1.call-start = ((), (), s32[]{:S(2)}) async-start(), calls=%async_computation.6 | async-start | bytes 1179648 | tf_op jit(solution)/shard_map/psum | solution.py:121
  245.3 1.9 copy-start.3
  248.3 339.0 %reduce-scatter.4.cloned.1.call-start = ((), (), s32[]{:S(2)}) async-start(), calls=%async_computation.7 | async-start | bytes 245760
  250.4 28.7 %collective-permute-start.3 = (bf16[128,192]{0,1:T(8,128)(2,1)S(1)}, bf16[128,192]{0,1:T(8,128)(2,1)S(1)}, u32[]{:S(2)}, u32[]{:S(2)}) collective-permute-start(bf16[128,192]{0,1:T(8,128)(2,1)S(1)} %fusion.51), channel_id=1, source_target_pairs={{4,0},{8,4},{12,8},{16,12},{20,16},{24,20},{28,24},{32,28},{36,32}... | collective-permute-start | bytes 147464 | tf_op jit(solution)/shard_map/ppermute | solution.py:15
  258.8 21.5 %collective-permute-start.4 = (bf16[128,192]{0,1:T(8,128)(2,1)S(1)}, bf16[128,192]{0,1:T(8,128)(2,1)S(1)}, u32[]{:S(2)}, u32[]{:S(2)}) collective-permute-start(bf16[128,192]{0,1:T(8,128)(2,1)S(1)} %fusion.52), channel_id=1, source_target_pairs={{4,0},{8,4},{12,8},{16,12},{20,16},{24,20},{28,24},{32,28},{36,32}... | collective-permute-start | bytes 147464 | tf_op jit(solution)/shard_map/ppermute | solution.py:15
Sparse Core Ops, SparseCore 0:
  249.1 338.2 all-reduce.1
Sparse Core Ops, SparseCore 1:
  260.8 27.3 reduce-scatter.3
where the time goes:
time: 598 us; the launch traced here: 597 us
  waiting for transfers between devices  418 us (70%)
  starting transfers between devices  67 us (11%)
  local copies, waits for them, and re-layouts  39.3 us (7%)
  other arithmetic  24.8 us (4%)
  matrix products  18.8 us (3%)
  between operations  17.4 us (3%)
  blocking collectives  11.4 us (2%)
    psum x1, waiting for transfers between devices, on_device(): weight_grad = lax.psum(weight_part, 'row')  292 us
    all_to_all x1, waiting for transfers between devices, on_device(): lax.all_to_all(jnp.take(key_table, asked_rows, axis=0), 'row', split_axis...  40.9 us
    all_to_all x1, waiting for transfers between devices, on_device(): lax.all_to_all(slot_keys.astype(jnp.bfloat16), 'row', split_axis=0, conca...  34.5 us
    ppermute x5, waiting for transfers between devices, shifted(): return lax.ppermute(block, axis, route)  26.5 us
    unnamed x40, local copies, waits for them, and re-layouts  23.9 us
    all_to_all x1, starting transfers between devices, on_device(): lax.all_to_all(asking.reshape(n_row, 1), 'row', split_axis=0, concat_axis...  20.4 us
    ppermute x5, starting transfers between devices, shifted(): return lax.ppermute(block, axis, route)  13.6 us
    all_to_all x1, waiting for transfers between devices, on_device(): lax.all_to_all(asking.reshape(n_row, 1), 'row', split_axis=0, concat_axis...  12.9 us
  transfers between devices with their start and end apart: 12, of which 7 were waited for; matrix products, arithmetic and copies ran while one was open for 9% of the time, Pallas kernels for 0%

commit v1 on v0

v1 whole, which is shorter than its diff:
```python
import jax
import jax.numpy as jnp
from jax import lax
from jax.experimental import pallas as pl
from jax.experimental.pallas import tpu as pltpu
from jax.sharding import Mesh, PartitionSpec as P

HEAD_DIM = 64
CELLS_BLK = 128
ROW_CELLS = 16
ROWS_BLK = 8
NX, NZ, NC = 4, 16, 2
ROW = ("x", "z", "c")
SIDE = ("x", "c")
NSIDE = NX * NC
SLOTS = NSIDE * NZ
KEYS = 2 * CELLS_BLK + SLOTS * ROW_CELLS


def shifted(block, distance):
    devices = range(NX * NZ * NC)
    route = [(i - distance, i) for i in devices if i - distance in devices]
    return lax.ppermute(block, ROW, route)


def attend_kernel(
    q_ref, da_ref, prior_ref, own_ref, slots_ref, seen_ref, att_ref, dq_ref, dprior_ref, down_ref, dslots_ref
):
    scale = HEAD_DIM ** (-0.5)
    kv = jnp.concatenate([prior_ref[...], own_ref[...], slots_ref[...]], axis=0)
    q, da = q_ref[...], da_ref[...]
    blank = jnp.zeros_like(q)
    both = jnp.concatenate(
        [jnp.concatenate([q, blank], axis=1), jnp.concatenate([blank, da], axis=1)], axis=0
    )
    cross = jnp.dot(kv, both, preferred_element_type=jnp.float32)
    visible = seen_ref[...] > 0.5
    scores = jnp.where(visible, cross[:, :CELLS_BLK] * scale, -1e30)
    top = jnp.max(scores, axis=0, keepdims=True)
    grown = jnp.where(visible, jnp.exp(scores - top), 0.0)
    probs = grown / jnp.sum(grown, axis=0, keepdims=True)
    probs_low = probs.astype(jnp.bfloat16)
    d_probs = cross[:, CELLS_BLK:]
    delta = jnp.sum(probs * d_probs, axis=0, keepdims=True)
    d_scores = (probs * (d_probs - delta) * scale).astype(jnp.bfloat16)
    pair = jnp.concatenate([d_scores, probs_low], axis=1)
    d_kv = lax.dot_general(pair, both, (((1,), (1,)), ((), ())), preferred_element_type=jnp.float32)
    mixed = lax.dot_general(kv, pair, (((0,), (0,)), ((), ())), preferred_element_type=jnp.float32)
    dq_ref[...] = mixed[:HEAD_DIM, :CELLS_BLK].astype(jnp.bfloat16)
    att_ref[...] = mixed[HEAD_DIM:, CELLS_BLK:].astype(jnp.bfloat16)
    dprior_ref[...] = d_kv[:CELLS_BLK].astype(jnp.bfloat16)
    down_ref[...] = d_kv[CELLS_BLK : 2 * CELLS_BLK]
    dslots_ref[...] = d_kv[2 * CELLS_BLK :].astype(jnp.bfloat16)


def attend(q, da, prior, own, slots, seen):
    heads = q.shape[0] // HEAD_DIM
    width = own.shape[1]
    feat = pl.BlockSpec((HEAD_DIM, CELLS_BLK), lambda h: (h, 0))
    cells = pl.BlockSpec((CELLS_BLK, 2 * HEAD_DIM), lambda h: (0, h))
    many = pl.BlockSpec((SLOTS * ROW_CELLS, 2 * HEAD_DIM), lambda h: (0, h))
    bf, f32 = jnp.bfloat16, jnp.float32
    return pl.pallas_call(
        attend_kernel,
        grid=(heads,),
        in_specs=[feat, feat, cells, cells, many, pl.BlockSpec((KEYS, 1), lambda h: (0, 0))],
        out_specs=[feat, feat, cells, cells, many],
        out_shape=[
            jax.ShapeDtypeStruct(q.shape, bf),
            jax.ShapeDtypeStruct(q.shape, bf),
            jax.ShapeDtypeStruct((CELLS_BLK, width), bf),
            jax.ShapeDtypeStruct((CELLS_BLK, width), f32),
            jax.ShapeDtypeStruct((SLOTS * ROW_CELLS, width), bf),
        ],
        name="attend",
    )(q, da, prior, own, slots, seen)


def pick_kernel(index_ref, table_ref, out_ref):
    for peer in range(NSIDE):
        for z in range(NZ):
            out_ref[peer, z] = table_ref[z, index_ref[peer, z]]


def pick(index, table):
    return pl.pallas_call(
        pick_kernel,
        in_specs=[pl.BlockSpec(memory_space=pltpu.SMEM), pl.BlockSpec(memory_space=pltpu.VMEM)],
        out_specs=pl.BlockSpec(memory_space=pltpu.VMEM),
        out_shape=jax.ShapeDtypeStruct((NSIDE, NZ) + table.shape[2:], table.dtype),
        name="pick",
    )(index, table)


def gather_back_kernel(index_ref, parts_ref, out_ref, total):
    for z in range(NZ):
        total[...] = jnp.zeros_like(total)
        for peer in range(NSIDE):
            spot = index_ref[peer, z]
            total[spot] = total[spot] + parts_ref[peer, z].astype(jnp.float32)
        out_ref[z] = total[...].astype(out_ref.dtype)


def gather_back(index, parts):
    tail = parts.shape[2:]
    return pl.pallas_call(
        gather_back_kernel,
        in_specs=[pl.BlockSpec(memory_space=pltpu.SMEM), pl.BlockSpec(memory_space=pltpu.VMEM)],
        out_specs=pl.BlockSpec(memory_space=pltpu.VMEM),
        out_shape=jax.ShapeDtypeStruct((NZ, ROWS_BLK) + tail, parts.dtype),
        scratch_shapes=[pltpu.VMEM((ROWS_BLK,) + tail, jnp.float32)],
        name="gather_back",
    )(index, parts)


def on_device(
    queries, key_cells, value_cells, out_weight, out_cotangent, parent_rows, window_reach, valid_cells
):
    bf, f32 = jnp.bfloat16, jnp.float32
    features = queries.shape[0]
    heads = features // HEAD_DIM
    width = 2 * features
    x_at, z_at, c_at = (lax.axis_index(name) for name in ROW)
    block_id = (x_at * NZ + z_at) * NC + c_at
    valid = valid_cells[0]
    pairs = jnp.concatenate(
        [key_cells.reshape(heads, HEAD_DIM, -1), value_cells.reshape(heads, HEAD_DIM, -1)], axis=1
    )
    own = pairs.reshape(width, CELLS_BLK).T
    table = lax.all_gather(own.reshape(ROWS_BLK, ROW_CELLS, width), "z")
    told = jnp.full((ROW_CELLS, width), valid.astype(bf))
    from_prior = shifted(jnp.concatenate([own, told], axis=0), 1)
    prior = from_prior[:CELLS_BLK]
    prior_valid = from_prior[CELLS_BLK, 0].astype(jnp.int32)

    wanted = parent_rows.reshape(-1)
    asked = lax.all_gather(wanted, SIDE)
    owner_here = (x_at * NZ + jnp.arange(NZ)) * NC + c_at
    hit = (asked // ROWS_BLK)[:, None, :] == owner_here[None, :, None]
    index = jnp.sum(jnp.where(hit, (asked % ROWS_BLK)[:, None, :], 0), axis=-1)
    side_ids = jnp.arange(NSIDE)
    slot_owner = ((side_ids // NC)[:, None] * NZ + jnp.arange(NZ)[None, :]) * NC + (side_ids % NC)[:, None]
    slot_seen = jnp.any(slot_owner.reshape(-1)[:, None] == (wanted // ROWS_BLK)[None, :], axis=-1)
    cell_ids = jnp.arange(CELLS_BLK)
    prior_seen = (cell_ids < prior_valid) & (window_reach[0] == 1) & (block_id > 0)
    seen = jnp.concatenate([prior_seen, cell_ids < valid, jnp.repeat(slot_seen, ROW_CELLS)])
    seen = seen.astype(f32)[:, None]

    slots = lax.all_to_all(pick(index, table), SIDE, split_axis=0, concat_axis=0, tiled=True)
    cotangent_all = lax.all_gather(out_cotangent, "mp", axis=0, tiled=True)
    d_attended = jnp.dot(out_weight, cotangent_all, preferred_element_type=f32).astype(bf)
    attended, d_queries, d_prior, d_own, d_slots = attend(
        queries, d_attended, prior, own, slots.reshape(SLOTS * ROW_CELLS, width), seen
    )
    parts = lax.all_to_all(
        d_slots.reshape(NSIDE, NZ, ROW_CELLS, width), SIDE, split_axis=0, concat_axis=0, tiled=True
    )
    returned = shifted(d_prior, -1)
    weight_part = lax.dot_general(
        attended, cotangent_all, (((1,), (1,)), ((), ())), preferred_element_type=f32
    )
    depth = features // NSIDE
    weight_split = lax.all_to_all(
        weight_part.astype(bf).reshape(NSIDE, depth, -1), SIDE, split_axis=0, concat_axis=0, tiled=True
    )
    weight_mine = lax.psum(jnp.sum(weight_split.astype(f32), axis=0), "z")
    weight_grad = lax.all_gather(weight_mine, SIDE, axis=0, tiled=True)
    partial_out = lax.dot_general(
        out_weight, attended, (((0,), (0,)), ((), ())), preferred_element_type=f32
    )
    mixed = lax.psum_scatter(partial_out.astype(bf), "mp", scatter_dimension=0, tiled=True)
    owner_parts = lax.psum_scatter(gather_back(index, parts), "z", scatter_dimension=0, tiled=False)
    total = d_own + returned.astype(f32) + owner_parts.reshape(CELLS_BLK, width).astype(f32)
    d_pairs = total.astype(bf).T.reshape(heads, 2, HEAD_DIM, CELLS_BLK)
    d_key_cells = d_pairs[:, 0].reshape(features, CELLS_BLK)
    d_value_cells = d_pairs[:, 1].reshape(features, CELLS_BLK)
    return mixed, d_queries, d_key_cells, d_value_cells, weight_grad


def solution(mesh):
    fine = Mesh(mesh.devices.reshape(NX, NZ, NC, -1), ROW + ("mp",))
    split = P("mp", ROW)
    return jax.shard_map(
        on_device,
        mesh=fine,
        in_specs=(split, split, split, P("mp", None), split, P(ROW, None), P(ROW), P(ROW)),
        out_specs=(split, split, split, split, P("mp", None)),
        check_vma=False,
    )
```

time: 598 us -> 383 us (0.64)
  waiting for transfers between devices: 418 us -> 251 us
  blocking collectives: 11.4 us -> 56.2 us
  starting transfers between devices: 67 us -> 26.6 us
  local copies, waits for them, and re-layouts: 39.3 us -> 10.1 us
  other arithmetic: 24.8 us -> 3.56 us
  matrix products: 18.8 us -> 2.12 us
  Pallas kernels: 0 us -> 15.5 us
    psum x1, waiting for transfers between devices: 292 us -> 93.5 us  [on_device(): weight_mine = lax.psum(jnp.sum(weight_split.astype(f32), axis=0), 'z')]
    all_to_all x5 -> x2, waiting for transfers between devices: 99.3 us -> 25.5 us  [the longest x1 20 us: on_device(): lax.all_to_all(d_slots.reshape(NSIDE, NZ, ROW_CELLS, width), SIDE, split_...]
    all_gather x0 -> x1, waiting for transfers between devices: none -> 50.1 us  [on_device(): table = lax.all_gather(own.reshape(ROWS_BLK, ROW_CELLS, width), 'z')]
    reduce_scatter x0 -> x1, waiting for transfers between devices: none -> 46.5 us  [on_device(): lax.psum_scatter(gather_back(index, parts), 'z', scatter_dimension=0, til...]
    unnamed x3 -> x5, waiting for transfers between devices: 0.04 us -> 35.5 us
    all_gather x0 -> x2, blocking collectives: none -> 35.2 us  [the longest x1 24.2 us: on_device(): weight_grad = lax.all_gather(weight_mine, SIDE, axis=0, tiled=True)]
    all_to_all x5 -> x2, starting transfers between devices: 53.2 us -> 18.8 us  [the longest x1 14.7 us: on_device(): lax.all_to_all(pick(index, table), SIDE, split_axis=0, concat_axis=0, til...]
    ppermute x5 -> x2, waiting for transfers between devices: 26.5 us -> 0.01 us  [shifted(): return lax.ppermute(block, ROW, route)]
  transfers between devices with their start and end apart: 12 -> 8, of which waited for: 7 -> 6; matrix products, arithmetic and copies ran while one was open for 9% -> 2% of each run, Pallas kernels for 0% -> 2%
where the time goes in v1:
time: 383 us; the launch traced here: 381 us
  waiting for transfers between devices  251 us (66%)
  blocking collectives  56.2 us (15%)
  starting transfers between devices  26.6 us (7%)
  between operations  15.9 us (4%)
  Pallas kernels  15.5 us (4%)
  local copies, waits for them, and re-layouts  10.1 us (3%)
    psum x1, waiting for transfers between devices, on_device(): weight_mine = lax.psum(jnp.sum(weight_split.astype(f32), axis=0), 'z')  93.5 us
    all_gather x1, waiting for transfers between devices, on_device(): table = lax.all_gather(own.reshape(ROWS_BLK, ROW_CELLS, width), 'z')  50.1 us
    reduce_scatter x1, waiting for transfers between devices, on_device(): lax.psum_scatter(gather_back(index, parts), 'z', scatter_dimension=0, til...  46.5 us
    unnamed x5, waiting for transfers between devices  35.5 us
    all_gather x1, blocking collectives, on_device(): weight_grad = lax.all_gather(weight_mine, SIDE, axis=0, tiled=True)  24.2 us
    all_to_all x1, waiting for transfers between devices, on_device(): lax.all_to_all(d_slots.reshape(NSIDE, NZ, ROW_CELLS, width), SIDE, split_...  20 us
    all_to_all x1, starting transfers between devices, on_device(): lax.all_to_all(pick(index, table), SIDE, split_axis=0, concat_axis=0, til...  14.7 us
    all_gather x1, blocking collectives, on_device(): asked = lax.all_gather(wanted, SIDE)  11 us
  transfers between devices with their start and end apart: 8, of which 6 were waited for; matrix products, arithmetic and copies ran while one was open for 2% of the time, Pallas kernels for 2%

profile of v1, /device:TPU:1, one launch (start us, length us, event | category | flops | bytes accessed | tf_op | source)
XLA Modules:
  0.0 381.1 jit_solution(8411439228079798473)
XLA Ops:
  7.2 0.0 all-gather.3.cloned.1.call-start
  7.2 0.9 pad_maximum_fusion
  8.1 0.8 copy.34
  8.8 0.0 all-gather.3.cloned.1.call-update
  9.5 0.9 concatenate.23
  10.4 4.9 %collective-permute-start = (bf16[144,384]{1,0:T(8,128)(2,1)S(1)}, bf16[144,384]{1,0:T(8,128)(2,1)S(1)}, u32[]{:S(2)}, u32[]{:S(2)}) collective-permute-start(bf16[144,384]{1,0:T(8,128)(2,1)S(1)} %concatenate.23), channel_id=1, source_target_pairs={{0,4},{4,8},{8,12},{12,16},{16,20},{20,24},{24,28},{28,32},{32,36}... | collective-permute-start | bytes 331784 | tf_op jit(solution)/shard_map/ppermute | solution.py:23
  16.0 11.0 %all-gather = s32[8,1,64]{2,1,0:T(1,128)S(1)} all-gather(s32[1,1,64]{2,1,0:T(1,128)} %bitcast.53), channel_id=1, replica_groups=mesh['x'=4,'z'=16,'c'=2,'mp'=4] {'x','c'}, dimensions={0}, use_global_device_ids=true | all-gather | bytes 2304 | tf_op jit(solution)/shard_map/all_gather | solution.py:137
  27.1 0.9 select_reduce_fusion.index_ref
  28.0 50.1 %all-gather.3.cloned.1.call-done.table_ref = bf16[16,8,16,384]{3,2,1,0:T(8,128)(2,1)} async-done(((bf16[1,8,16,384]{3,2,1,0:T(8,128)(2,1)}), bf16[16,8,16,384]{3,2,1,0:T(8,128)(2,1)}) %all-gather.3.cloned.1.call-update) | async-done | bytes 1572880 | tf_op jit(solution)/shard_map/all_gather | solution.py:130
  78.0 2.8 pick.1
  80.8 14.7 %all-to-all-start = ((bf16[8,16,16,384]{3,2,1,0:T(8,128)(2,1)}), bf16[8,16,16,384]{3,2,1,0:T(8,128)(2,1)S(1)}, u32[]{:S(2)}, u32[]{:S(2)}) async-start(bf16[8,16,16,384]{3,2,1,0:T(8,128)(2,1)} %pick.1), calls=%async_computation | async-start | bytes 3145728 | tf_op jit(solution)/shard_map/all_to_all | solution.py:149
  95.5 0.1 multiply_add_fusion
  95.6 0.1 add.110
  95.7 0.1 compare_reduce_fusion
  95.8 0.1 broadcast_in_dim.16
  95.9 0.1 concatenate.26
  96.0 10.5 %all_gather.12 = bf16[768,128]{1,0:T(8,128)(2,1)S(1)} all-gather(bf16[192,128]{1,0:T(8,128)(2,1)S(1)} %copy-done.5), channel_id=1, replica_groups=mesh['x'=4,'z'=16,'c'=2,'mp'=4] {'mp'}, dimensions={0}, use_global_device_ids=true | all-gather | bytes 245760 | tf_op jit(solution)/shard_map/all_gather | solution.py:150
  106.5 0.9 convolution_convert_fusion.2.da_ref
  107.3 0.5 slice.17
  108.5 1.4 copy.35.seen_ref
  110.0 0.7 slice.16.prior_ref
  110.7 5.6 %all-to-all-done = bf16[8,16,16,384]{3,2,1,0:T(8,128)(2,1)S(1)} async-done(((bf16[8,16,16,384]{3,2,1,0:T(8,128)(2,1)}), bf16[8,16,16,384]{3,2,1,0:T(8,128)(2,1)S(1)}, u32[]{:S(2)}, u32[]{:S(2)}) %all-to-all-start) | async-done | bytes 1572896 | tf_op jit(solution)/shard_map/all_to_all | solution.py:149
  116.3 1.1 copy-done.1
  117.4 9.1 %attend.1 = (bf16[192,128]{1,0:T(8,128)(2,1)}, bf16[192,128]{1,0:T(8,128)(2,1)}, bf16[128,384]{1,0:T(8,128)(2,1)}, f32[128,384]{1,0:T(8,128)}, bf16[2048,384]{1,0:T(8,128)(2,1)}) custom-call(bf16[192,128]{1,0:T(8,128)(2,1)} %q_ref.1, bf16[192,128]{1,0:T(8,128)(2,1)} %convolution_convert_fusion.2.da_ref, bf16[128,384]{1,0:T(8,128)(2,1)} %slice.16.prior_ref, ...), custom_call_target="tpu_custom_call" | custom-call | tf_op jit(solution)/shard_map/attend/pallas_call | solution.py:63
  126.5 1.0 convolution_convert_fusion
  127.6 10.6 %all_to_all.15 = bf16[8,24,768]{2,1,0:T(8,128)(2,1)S(1)} all-to-all(bf16[8,24,768]{2,1,0:T(8,128)(2,1)S(1)} %bitcast.45), channel_id=1, replica_groups=mesh['x'=4,'z'=16,'c'=2,'mp'=4] {'x','c'}, dimensions={0} | all-to-all | bytes 589824 | tf_op jit(solution)/shard_map/all_to_all | solution.py:163
  138.1 4.1 %all-to-all-start.1 = ((bf16[8,16,16,384]{3,2,1,0:T(8,128)(2,1)}), bf16[8,16,16,384]{3,2,1,0:T(8,128)(2,1)S(1)}, u32[]{:S(2)}, u32[]{:S(2)}) async-start(bf16[8,16,16,384]{3,2,1,0:T(8,128)(2,1)} %bitcast.44), calls=%async_computation.1 | async-start | bytes 3145728 | tf_op jit(solution)/shard_map/all_to_all | solution.py:155
  142.2 0.7 convert_reduce_fusion
  142.8 0.1 all-reduce.3.cloned.1.call-update
  142.9 0.0 reduce-scatter.5.cloned.1.call-start
  143.0 20.0 %all-to-all-done.1.parts_ref = bf16[8,16,16,384]{3,2,1,0:T(8,128)(2,1)S(1)} async-done(((bf16[8,16,16,384]{3,2,1,0:T(8,128)(2,1)}), bf16[8,16,16,384]{3,2,1,0:T(8,128)(2,1)S(1)}, u32[]{:S(2)}, u32[]{:S(2)}) %all-to-all-start.1) | async-done | bytes 1572896 | tf_op jit(solution)/shard_map/all_to_all | solution.py:155
  162.9 1.1 copy-done.2
  164.1 3.6 gather_back.1
  167.7 0.0 reduce-scatter.5.cloned.1.call-update
  167.7 0.0 reduce-scatter.7.cloned.1.call-start
  167.8 0.8 copy-done.7
  168.6 2.8 collective-permute-start.1
  171.4 0.2 fusion
  171.6 0.8 copy.38
  172.4 0.0 reduce-scatter.7.cloned.1.call-update
  172.5 93.5 %all-reduce.3.cloned.1.call-done = f32[24,768]{1,0:T(8,128)} async-done(((f32[24,768]{1,0:T(8,128)}), f32[24,768]{1,0:T(8,128)}) %all-reduce.3.cloned.1.call-update) | async-done | bytes 73744 | tf_op jit(solution)/shard_map/psum | solution.py:166
  266.0 24.2 %all_gather.15 = f32[192,768]{1,0:T(8,128)S(1)} all-gather(f32[24,768]{1,0:T(8,128)} %all-reduce.3.cloned.1.call-done), channel_id=1, replica_groups=mesh['x'=4,'z'=16,'c'=2,'mp'=4] {'x','c'}, dimensions={0}, use_global_device_ids=true | all-gather | bytes 663552 | tf_op jit(solution)/shard_map/all_gather | solution.py:167
  290.1 46.5 %reduce-scatter.5.cloned.1.call-done = bf16[1,8,16,384]{3,2,1,0:T(8,128)(2,1)} async-done(((bf16[16,8,16,384]{3,2,1,0:T(8,128)(2,1)}), bf16[1,8,16,384]{3,2,1,0:T(8,128)(2,1)}) %reduce-scatter.5.cloned.1.call-update) | async-done | bytes 98320 | tf_op jit(solution)/shard_map/reduce_scatter | solution.py:172
  336.6 0.9 fusion.2
  337.5 0.1 copy.36
  337.7 0.6 fusion.7
  338.3 35.4 %reduce-scatter.7.cloned.1.call-done = bf16[192,128]{1,0:T(8,128)(2,1)} async-done(((bf16[768,128]{1,0:T(8,128)(2,1)}), bf16[192,128]{1,0:T(8,128)(2,1)}) %reduce-scatter.7.cloned.1.call-update) | async-done | bytes 49168
  373.7 0.8 copy.44
  (23 shorter events, 0.1 us)
Async XLA Ops:
  7.2 99.3 %copy-start = (bf16[192,768]{1,0:T(8,128)(2,1)S(1)}, bf16[192,768]{1,0:T(8,128)(2,1)}, u32[]{:S(2)}) copy-start(bf16[192,768]{1,0:T(8,128)(2,1)} %param.11) | copy-start | bytes 884740
  7.2 70.9 %all-gather.3.cloned.1.call-start = ((), (), s32[]{:S(2)}) async-start(), calls=%async_computation.5 | async-start | bytes 1671168 | tf_op jit(solution)/shard_map/all_gather | solution.py:130
  10.4 96.9 %collective-permute-start = (bf16[144,384]{1,0:T(8,128)(2,1)S(1)}, bf16[144,384]{1,0:T(8,128)(2,1)S(1)}, u32[]{:S(2)}, u32[]{:S(2)}) collective-permute-start(bf16[144,384]{1,0:T(8,128)(2,1)S(1)} %concatenate.23), channel_id=1, source_target_pairs={{0,4},{4,8},{8,12},{12,16},{16,20},{20,24},{24,28},{28,32},{32,36}... | collective-permute-start | bytes 331784 | tf_op jit(solution)/shard_map/ppermute | solution.py:23
  80.8 14.9 %copy-start.6 = (s32[1,64]{1,0:T(1,128)S(1)}, s32[1,64]{1,0:T(1,128)}, u32[]{:S(2)}) copy-start(s32[1,64]{1,0:T(1,128)} %param.13) | copy-start | bytes 772
  80.8 15.2 %copy-start.5 = (bf16[192,128]{1,0:T(8,128)(2,1)S(1)}, bf16[192,128]{1,0:T(8,128)(2,1)}, u32[]{:S(2)}) copy-start(bf16[192,128]{1,0:T(8,128)(2,1)} %param.12) | copy-start | bytes 147460
  80.8 35.4 %all-to-all-start = ((bf16[8,16,16,384]{3,2,1,0:T(8,128)(2,1)}), bf16[8,16,16,384]{3,2,1,0:T(8,128)(2,1)S(1)}, u32[]{:S(2)}, u32[]{:S(2)}) async-start(bf16[8,16,16,384]{3,2,1,0:T(8,128)(2,1)} %pick.1), calls=%async_computation | async-start | bytes 3145728 | tf_op jit(solution)/shard_map/all_to_all | solution.py:149
  116.3 1.1 copy-start.1
  138.1 24.8 %all-to-all-start.1 = ((bf16[8,16,16,384]{3,2,1,0:T(8,128)(2,1)}), bf16[8,16,16,384]{3,2,1,0:T(8,128)(2,1)S(1)}, u32[]{:S(2)}, u32[]{:S(2)}) async-start(bf16[8,16,16,384]{3,2,1,0:T(8,128)(2,1)} %bitcast.44), calls=%async_computation.1 | async-start | bytes 3145728 | tf_op jit(solution)/shard_map/all_to_all | solution.py:155
  142.2 123.8 %all-reduce.3.cloned.1.call-start = ((), (), s32[]{:S(2)}) async-start(), calls=%async_computation.7 | async-start | bytes 147456 | tf_op jit(solution)/shard_map/psum | solution.py:166
  142.9 193.7 %reduce-scatter.5.cloned.1.call-start = ((), (), s32[]{:S(2)}) async-start(), calls=%async_computation.6 | async-start | bytes 1671168 | tf_op jit(solution)/shard_map/reduce_scatter | solution.py:172
  162.9 1.1 copy-start.2
  167.7 0.9 copy-start.7
  167.7 3.7 copy-start.3
  167.7 168.9 %copy-start.4 = (f32[128,384]{1,0:T(8,128)S(1)}, f32[128,384]{1,0:T(8,128)}, u32[]{:S(2)}) copy-start(f32[128,384]{1,0:T(8,128)} %get-tuple-element.12) | copy-start | bytes 589828
  167.7 206.0 %reduce-scatter.7.cloned.1.call-start = ((), (), s32[]{:S(2)}) async-start(), calls=%async_computation.8 | async-start | bytes 245760
  168.6 121.6 %collective-permute-start.1 = (bf16[128,384]{1,0:T(8,128)(2,1)S(1)}, bf16[128,384]{1,0:T(8,128)(2,1)S(1)}, u32[]{:S(2)}, u32[]{:S(2)}) collective-permute-start(bf16[128,384]{1,0:T(8,128)(2,1)S(1)} %copy-done.7), channel_id=1, source_target_pairs={{4,0},{8,4},{12,8},{16,12},{20,16},{24,20},{28,24},{32,28},{36,32}... | collective-permute-start | bytes 294920 | tf_op jit(solution)/shard_map/ppermute | solution.py:23
Sparse Core Ops, SparseCore 0:
  10.1 67.9 all-gather.2
  145.3 120.6 all-reduce.2
  269.1 67.4 reduce-scatter.4
  339.8 33.8 reduce-scatter.6

commit v2 on v1

--- a/solution.py
+++ b/solution.py
@@ -1,3 +1,5 @@
+import functools
+
 import jax
 import jax.numpy as jnp
 from jax import lax
@@ -11,16 +13,9 @@
 ROWS_BLK = 8
 NX, NZ, NC = 4, 16, 2
 ROW = ("x", "z", "c")
-SIDE = ("x", "c")
 NSIDE = NX * NC
 SLOTS = NSIDE * NZ
 KEYS = 2 * CELLS_BLK + SLOTS * ROW_CELLS
-
-
-def shifted(block, distance):
-    devices = range(NX * NZ * NC)
-    route = [(i - distance, i) for i in devices if i - distance in devices]
-    return lax.ppermute(block, ROW, route)
 
 
 def attend_kernel(
@@ -76,41 +71,303 @@
     )(q, da, prior, own, slots, seen)
 
 
-def pick_kernel(index_ref, table_ref, out_ref):
-    for peer in range(NSIDE):
+MESH = pl.DeviceIdType.MESH
+HOPS = (NZ // 2, NZ - NZ // 2 - 1)
+HALF = ROWS_BLK // 2
+SPARE = 16
+
+
+def remote(source, target, sems, spot, device):
+    return pltpu.make_async_remote_copy(
+        src_ref=source,
+        dst_ref=target,
+        send_sem=sems[0].at[spot],
+        recv_sem=sems[1].at[spot],
+        device_id=device,
+        device_id_type=MESH,
+    )
+
+
+def step_round(place, distance, size):
+    return lax.rem(place + (distance % size), size)
+
+
+def side_device(side):
+    return {"x": lax.div(side, NC), "c": lax.rem(side, NC)}
+
+
+def line_device(x, z, c, distance):
+    line = step_round((x * NZ + z) * NC + c, distance, NX * NZ * NC)
+    return {"x": lax.div(line, NZ * NC), "z": lax.rem(lax.div(line, NC), NZ), "c": lax.rem(line, NC)}
+
+
+def meet(peers):
+    barrier = pltpu.get_barrier_semaphore()
+    for peer in peers:
+        pl.semaphore_signal(barrier, inc=1, device_id=peer, device_id_type=MESH)
+    pl.semaphore_wait(barrier, len(peers))
+
+
+def side_peers(side):
+    return [side_device(step_round(side, d, NSIDE)) for d in range(1, NSIDE)]
+
+
+def fetch_kernel(
+    nmp, own_ref, info_ref, cot_ref, table_ref, asked_ref, cots_ref, prior_ref, told_ref,
+    ring_send, ring_recv, side_send, side_recv, mp_send, mp_recv, line_send, line_recv,
+):
+    x, z, c, mp = (lax.axis_index(name) for name in ROW + ("mp",))
+    side = x * NC + c
+    ways = [{"z": step_round(z, 1, NZ)}, {"z": step_round(z, -1, NZ)}]
+    after, before = line_device(x, z, c, 1), line_device(x, z, c, -1)
+    mp_peers = [{"mp": step_round(mp, d, nmp)} for d in range(1, nmp)]
+    meet(ways + side_peers(side) + mp_peers + [after, before])
+    ring = {}
+
+    def hop(way, s, half):
+        rows = pl.ds(half * HALF, HALF)
+        block = step_round(z, s if way else -s, NZ)
+        source = table_ref.at[block, rows] if s else own_ref.at[rows]
+        copy = remote(source, table_ref.at[block, rows], (ring_send, ring_recv), (way, s, half), ways[way])
+        copy.start()
+        ring[way, s, half] = copy
+
+    for half in range(2):
+        for way in range(2):
+            hop(way, 0, half)
+    others = []
+    for d, peer in enumerate(side_peers(side)):
+        others.append(remote(info_ref, asked_ref.at[side], (side_send, side_recv), d, peer))
+    for d, peer in enumerate(mp_peers):
+        others.append(remote(cot_ref, cots_ref.at[mp], (mp_send, mp_recv), d, peer))
+    others.append(remote(own_ref, prior_ref, (line_send, line_recv), 0, after))
+    others.append(remote(info_ref, told_ref, (line_send, line_recv), 1, after))
+    for copy in others:
+        copy.start()
+    table_ref[z] = own_ref[...]
+    asked_ref[side] = info_ref[...]
+    cots_ref[mp] = cot_ref[...]
+    for s in range(1, HOPS[0]):
+        for half in range(2):
+            for way in range(2):
+                if s < HOPS[way]:
+                    ring[way, s - 1, half].wait_recv()
+                    hop(way, s, half)
+    for half in range(2):
+        for way in range(2):
+            ring[way, HOPS[way] - 1, half].wait_recv()
+    for copy in others:
+        copy.wait()
+    for copy in ring.values():
+        copy.wait_send()
+
+
+def vmem():
+    return pl.BlockSpec(memory_space=pltpu.VMEM)
+
+
+def pair_sems(*shape):
+    return [pltpu.SemaphoreType.DMA(shape), pltpu.SemaphoreType.DMA(shape)]
+
+
+def fetch(own, info, cot, nmp):
+    bf, i32 = jnp.bfloat16, jnp.int32
+    shapes = [
+        ((NZ,) + own.shape, bf),
+        ((NSIDE,) + info.shape, i32),
+        ((nmp,) + cot.shape, bf),
+        (own.shape, bf),
+        (info.shape, i32),
+    ]
+    return pl.pallas_call(
+        functools.partial(fetch_kernel, nmp),
+        in_specs=[vmem()] * 3,
+        out_specs=[vmem()] * 5,
+        out_shape=[jax.ShapeDtypeStruct(*shape) for shape in shapes],
+        scratch_shapes=pair_sems(2, HOPS[0], 2) + pair_sems(NSIDE - 1) + pair_sems(nmp - 1) + pair_sems(2),
+        compiler_params=pltpu.CompilerParams(collective_id=0, has_side_effects=True),
+        name="fetch",
+    )(own, info, cot)
+
+
+def spread_kernel(index_ref, table_ref, slots_ref, held, side_send, side_recv):
+    side = lax.axis_index("x") * NC + lax.axis_index("c")
+    peers = side_peers(side)
+    meet(peers)
+    copies = []
+    for d in FAR_FIRST:
+        to = step_round(side, d + 1, NSIDE)
         for z in range(NZ):
-            out_ref[peer, z] = table_ref[z, index_ref[peer, z]]
-
-
-def pick(index, table):
+            held[d, z] = table_ref[z, index_ref[to, z]]
+        copy = remote(held.at[d], slots_ref.at[side], (side_send, side_recv), d, peers[d])
+        copy.start()
+        copies.append(copy)
+    for z in range(NZ):
+        slots_ref[side, z] = table_ref[z, index_ref[side, z]]
+    for copy in copies:
+        copy.wait()
+
+
+FAR_FIRST = (3, 2, 4, 1, 5, 0, 6)
+
+
+def spread(index, table):
+    tail = table.shape[2:]
     return pl.pallas_call(
-        pick_kernel,
-        in_specs=[pl.BlockSpec(memory_space=pltpu.SMEM), pl.BlockSpec(memory_space=pltpu.VMEM)],
-        out_specs=pl.BlockSpec(memory_space=pltpu.VMEM),
-        out_shape=jax.ShapeDtypeStruct((NSIDE, NZ) + table.shape[2:], table.dtype),
-        name="pick",
+        spread_kernel,
+        in_specs=[pl.BlockSpec(memory_space=pltpu.SMEM), vmem()],
+        out_specs=vmem(),
+        out_shape=jax.ShapeDtypeStruct((NSIDE, NZ) + tail, table.dtype),
+        scratch_shapes=[pltpu.VMEM((NSIDE - 1, NZ) + tail, table.dtype)] + pair_sems(NSIDE - 1),
+        compiler_params=pltpu.CompilerParams(collective_id=1, has_side_effects=True),
+        name="spread",
     )(index, table)
 
 
-def gather_back_kernel(index_ref, parts_ref, out_ref, total):
-    for z in range(NZ):
-        total[...] = jnp.zeros_like(total)
-        for peer in range(NSIDE):
-            spot = index_ref[peer, z]
-            total[spot] = total[spot] + parts_ref[peer, z].astype(jnp.float32)
-        out_ref[z] = total[...].astype(out_ref.dtype)
-
-
-def gather_back(index, parts):
-    tail = parts.shape[2:]
+def settle_kernel(
+    nmp, index_ref, slots_ref, dprior_ref, down_ref, out_ref, weight_ref, total_ref, mixed_ref, wall_ref,
+    parts, share, sent, got, back, mixes, wside, wsum, wz, wone, wring,
+    ring_send, ring_recv, side_send, side_recv, mp_send, mp_recv, line_send, line_recv,
+    w1_send, w1_recv, w2_send, w2_recv, w3_send, w3_recv, w4_send, w4_recv,
+):
+    bf, f32 = jnp.bfloat16, jnp.float32
+    x, z, c, mp = (lax.axis_index(name) for name in ROW + ("mp",))
+    side = x * NC + c
+    z_peers = [{"z": step_round(z, d, NZ)} for d in range(1, NZ)]
+    ways = [z_peers[0], z_peers[-1]]
+    after, before = line_device(x, z, c, 1), line_device(x, z, c, -1)
+    mp_peers = [{"mp": step_round(mp, d, nmp)} for d in range(1, nmp)]
+    peers = side_peers(side)
+    meet(z_peers + peers + mp_peers + [after, before])
+    side_copies, w1, others = [], [], []
+    for d in FAR_FIRST:
+        to = step_round(side, d + 1, NSIDE)
+        side_copies.append(remote(slots_ref.at[to], parts.at[side], (side_send, side_recv), d, peers[d]))
+        w1.append(remote(weight_ref.at[to], wside.at[side], (w1_send, w1_recv), d, peers[d]))
+    for d, peer in enumerate(mp_peers):
+        to = step_round(mp, d + 1, nmp)
+        others.append(remote(out_ref.at[to], mixes.at[mp], (mp_send, mp_recv), d, peer))
+    others.append(remote(dprior_ref, back, (line_send, line_recv), 0, before))
+    for copy in side_copies + w1 + others:
+        copy.start()
+    parts[side] = slots_ref[side]
+    wside[side] = weight_ref[side]
+    mixes[mp] = out_ref[mp]
+    for copy in side_copies:
+        copy.wait_recv()
+
+    def fill(t, carry):
+        for row in range(ROWS_BLK):
+            total = jnp.zeros(parts.shape[2:], f32)
+            for peer in range(NSIDE):
+                mark = jnp.where(index_ref[peer, t] == row, 1.0, 0.0)
+                total = total + parts[peer, t].astype(f32) * mark
+            share[t, row] = total
+        return carry
+
+    lax.fori_loop(0, NZ, fill, 0)
+    ring = {}
+    w2, w3, w4 = [], [], []
+    for s in range(HOPS[0]):
+        for half in range(2):
+            rows = pl.ds(half * HALF, HALF)
+            for way in range(2):
+                if s >= HOPS[way]:
+                    continue
+                target = step_round(z, s - HOPS[1] if way else HOPS[0] - s, NZ)
+                mine = share[target, rows]
+                if s:
+                    ring[way, s - 1, half].wait_recv()
+                    mine = mine + got[way, s - 1, rows].astype(f32)
+                sent[way, s, rows] = mine.astype(bf)
+                copy = remote(
+                    sent.at[way, s, rows], got.at[way, s, rows], (ring_send, ring_recv), (way, s, half), ways[way]
+                )
+                copy.start()
+                ring[way, s, half] = copy
+        if s == 0:
+            for copy in w1:
+                copy.wait_recv()
+            summed = wside[0].astype(f32)
+            for peer in range(1, NSIDE):
+                summed = summed + wside[peer].astype(f32)
+            wsum[...] = summed.astype(bf)
+            for d, peer in enumerate(z_peers):
+                to = step_round(z, d + 1, NZ)
+                w2.append(remote(wsum.at[to], wz.at[z], (w2_send, w2_recv), d, peer))
+                w2[-1].start()
+            wz[z] = wsum[z]
+        if s == 3:
+            for copy in w2:
+                copy.wait_recv()
+            one = wz[0].astype(f32)
+            for peer in range(1, NZ):
+                one = one + wz[peer].astype(f32)
+            wone[...] = one
+            for d, peer in enumerate(z_peers):
+                w3.append(remote(wone, wring.at[z], (w3_send, w3_recv), d, peer))
+                w3[-1].start()
+            wring[z] = wone[...]
+        if s == 6:
+            for copy in w3:
+                copy.wait_recv()
+            for d in FAR_FIRST:
+                w4.append(remote(wring, wall_ref.at[side], (w4_send, w4_recv), d, peers[d]))
+                w4[-1].start()
+            wall_ref[side] = wring[...]
+    for copy in others:
+        copy.wait()
+    mixed = mixes[0].astype(f32)
+    for peer in range(1, nmp):
+        mixed = mixed + mixes[peer].astype(f32)
+    mixed_ref[...] = mixed.astype(bf)
+    for half in range(2):
+        for way in range(2):
+            ring[way, HOPS[way] - 1, half].wait_recv()
+    total = down_ref[...] + back[...].astype(f32) + share[z]
+    for way in range(2):
+        total = total + got[way, HOPS[way] - 1].astype(f32)
+    total_ref[...] = total.astype(bf)
+    for copy in w4:
+        copy.wait()
+    for copy in list(ring.values()) + side_copies + w1 + w2 + w3:
+        copy.wait_send()
+
+
+def settle(index, slots, dprior, down, out, weight):
+    bf, f32 = jnp.bfloat16, jnp.float32
+    nmp = out.shape[0]
+    tail = slots.shape[2:]
+    block = (ROWS_BLK,) + tail
+    piece = weight.shape[1:]
+    scratch = [
+        (slots.shape, bf),
+        ((NZ,) + block, f32),
+        ((2, HOPS[0]) + block, bf),
+        ((2, HOPS[0]) + block, bf),
+        (block, bf),
+        (out.shape, bf),
+        (weight.shape, bf),
+        (piece, bf),
+        (piece, bf),
+        (piece[1:], f32),
+        (piece, f32),
+    ]
+    sems = pair_sems(2, HOPS[0], 2) + pair_sems(NSIDE - 1) + pair_sems(nmp - 1) + pair_sems(1)
+    sems += pair_sems(NSIDE - 1) + pair_sems(NZ - 1) + pair_sems(NZ - 1) + pair_sems(NSIDE - 1)
     return pl.pallas_call(
-        gather_back_kernel,
-        in_specs=[pl.BlockSpec(memory_space=pltpu.SMEM), pl.BlockSpec(memory_space=pltpu.VMEM)],
-        out_specs=pl.BlockSpec(memory_space=pltpu.VMEM),
-        out_shape=jax.ShapeDtypeStruct((NZ, ROWS_BLK) + tail, parts.dtype),
-        scratch_shapes=[pltpu.VMEM((ROWS_BLK,) + tail, jnp.float32)],
-        name="gather_back",
-    )(index, parts)
+        functools.partial(settle_kernel, nmp),
+        in_specs=[pl.BlockSpec(memory_space=pltpu.SMEM)] + [vmem()] * 5,
+        out_specs=[vmem()] * 3,
+        out_shape=[
+            jax.ShapeDtypeStruct(block, bf),
+            jax.ShapeDtypeStruct(out.shape[1:], bf),
+            jax.ShapeDtypeStruct(weight.shape, f32),
+        ],
+        scratch_shapes=[pltpu.VMEM(*shape) for shape in scratch] + sems,
+        compiler_params=pltpu.CompilerParams(collective_id=2, has_side_effects=True),
+        name="settle",
+    )(index, slots, dprior, down, out, weight)
 
 
 def on_device(
@@ -127,14 +384,17 @@
         [key_cells.reshape(heads, HEAD_DIM, -1), value_cells.reshape(heads, HEAD_DIM, -1)], axis=1
     )
     own = pairs.reshape(width, CELLS_BLK).T
-    table = lax.all_gather(own.reshape(ROWS_BLK, ROW_CELLS, width), "z")
-    told = jnp.full((ROW_CELLS, width), valid.astype(bf))
-    from_prior = shifted(jnp.concatenate([own, told], axis=0), 1)
-    prior = from_prior[:CELLS_BLK]
-    prior_valid = from_prior[CELLS_BLK, 0].astype(jnp.int32)
-
+    nmp = lax.axis_size("mp")
     wanted = parent_rows.reshape(-1)
-    asked = lax.all_gather(wanted, SIDE)
+    lanes = jnp.concatenate([wanted, valid_cells, jnp.zeros(127 - wanted.shape[0], jnp.int32)])
+    info = jnp.broadcast_to(lanes, (8, 128))
+    table, asked, cotangents, prior, told = fetch(
+        own.reshape(ROWS_BLK, ROW_CELLS, width), info, out_cotangent, nmp
+    )
+    cotangent_all = cotangents.reshape(-1, CELLS_BLK)
+    prior = prior.reshape(CELLS_BLK, width)
+    prior_valid = told[0, wanted.shape[0]]
+    asked = asked[:, 0, : wanted.shape[0]]
     owner_here = (x_at * NZ + jnp.arange(NZ)) * NC + c_at
     hit = (asked // ROWS_BLK)[:, None, :] == owner_here[None, :, None]
     index = jnp.sum(jnp.where(hit, (asked % ROWS_BLK)[:, None, :], 0), axis=-1)
@@ -146,32 +406,31 @@
     seen = jnp.concatenate([prior_seen, cell_ids < valid, jnp.repeat(slot_seen, ROW_CELLS)])
     seen = seen.astype(f32)[:, None]
 
-    slots = lax.all_to_all(pick(index, table), SIDE, split_axis=0, concat_axis=0, tiled=True)
-    cotangent_all = lax.all_gather(out_cotangent, "mp", axis=0, tiled=True)
+    slots = spread(index, table)
     d_attended = jnp.dot(out_weight, cotangent_all, preferred_element_type=f32).astype(bf)
     attended, d_queries, d_prior, d_own, d_slots = attend(
         queries, d_attended, prior, own, slots.reshape(SLOTS * ROW_CELLS, width), seen
     )
-    parts = lax.all_to_all(
-        d_slots.reshape(NSIDE, NZ, ROW_CELLS, width), SIDE, split_axis=0, concat_axis=0, tiled=True
-    )
-    returned = shifted(d_prior, -1)
     weight_part = lax.dot_general(
         attended, cotangent_all, (((1,), (1,)), ((), ())), preferred_element_type=f32
     )
-    depth = features // NSIDE
-    weight_split = lax.all_to_all(
-        weight_part.astype(bf).reshape(NSIDE, depth, -1), SIDE, split_axis=0, concat_axis=0, tiled=True
-    )
-    weight_mine = lax.psum(jnp.sum(weight_split.astype(f32), axis=0), "z")
-    weight_grad = lax.all_gather(weight_mine, SIDE, axis=0, tiled=True)
+    pieces = weight_part.astype(bf).reshape(NSIDE, NZ, -1, 128)
+    used = pieces.shape[2]
+    pieces = jnp.pad(pieces, ((0, 0), (0, 0), (0, SPARE - used), (0, 0)))
     partial_out = lax.dot_general(
         out_weight, attended, (((0,), (0,)), ((), ())), preferred_element_type=f32
     )
-    mixed = lax.psum_scatter(partial_out.astype(bf), "mp", scatter_dimension=0, tiled=True)
-    owner_parts = lax.psum_scatter(gather_back(index, parts), "z", scatter_dimension=0, tiled=False)
-    total = d_own + returned.astype(f32) + owner_parts.reshape(CELLS_BLK, width).astype(f32)
-    d_pairs = total.astype(bf).T.reshape(heads, 2, HEAD_DIM, CELLS_BLK)
+    block = (ROWS_BLK, ROW_CELLS, width)
+    total, mixed, weight_all = settle(
+        index,
+        d_slots.reshape(NSIDE, NZ, ROW_CELLS, width),
+        d_prior.reshape(block),
+        d_own.reshape(block),
+        partial_out.astype(bf).reshape(nmp, features, CELLS_BLK),
+        pieces,
+    )
+    weight_grad = weight_all[:, :, :used].reshape(features, -1)
+    d_pairs = total.reshape(CELLS_BLK, width).T.reshape(heads, 2, HEAD_DIM, CELLS_BLK)
     d_key_cells = d_pairs[:, 0].reshape(features, CELLS_BLK)
     d_value_cells = d_pairs[:, 1].reshape(features, CELLS_BLK)
     return mixed, d_queries, d_key_cells, d_value_cells, weight_grad

time: 383 us -> 172 us (0.45)
  waiting for transfers between devices: 251 us -> 0 us
  Pallas kernels: 15.5 us -> 150 us
  blocking collectives: 56.2 us -> 0 us
  starting transfers between devices: 26.6 us -> 0 us
  between operations: 15.9 us -> 2.11 us
    pallas_call x2 -> x3, Pallas kernels: 6.42 us -> 141 us  [the longest x1 71.1 us: settle(): pl.pallas_call(functools.partial(settle_kernel, nmp), in_specs=[pl.BlockS...]
    psum x1 -> x0, waiting for transfers between devices: 93.5 us -> none  [on_device(): weight_mine = lax.psum(jnp.sum(weight_split.astype(f32), axis=0), 'z')]
    all_gather x1 -> x0, waiting for transfers between devices: 50.1 us -> none  [on_device(): table = lax.all_gather(own.reshape(ROWS_BLK, ROW_CELLS, width), 'z')]
    reduce_scatter x1 -> x0, waiting for transfers between devices: 46.5 us -> none  [on_device(): lax.psum_scatter(gather_back(index, parts), 'z', scatter_dimension=0, til...]
    all_gather x3 -> x0, blocking collectives: 45.6 us -> none  [the longest x1 24.2 us: on_device(): weight_grad = lax.all_gather(weight_mine, SIDE, axis=0, tiled=True)]
    unnamed x5 -> x0, waiting for transfers between devices: 35.5 us -> none
    all_to_all x2 -> x0, waiting for transfers between devices: 25.5 us -> none  [the longest x1 20 us: on_device(): lax.all_to_all(d_slots.reshape(NSIDE, NZ, ROW_CELLS, width), SIDE, split_...]
    all_to_all x2 -> x0, starting transfers between devices: 18.8 us -> none  [the longest x1 14.7 us: on_device(): lax.all_to_all(pick(index, table), SIDE, split_axis=0, concat_axis=0, til...]
  transfers between devices with their start and end apart: 8 -> 0, of which waited for: 6 -> 0; matrix products, arithmetic and copies ran while one was open for 2% -> 0% of each run, Pallas kernels for 2% -> 0%
where the time goes in v2:
time: 172 us; the launch traced here: 171 us
  Pallas kernels  150 us (87%)
  local copies, waits for them, and re-layouts  10.8 us (6%)
  other arithmetic  4.74 us (3%)
  matrix products  2.9 us (2%)
  between operations  2.11 us (1%)
    pallas_call x1, Pallas kernels, settle(): pl.pallas_call(functools.partial(settle_kernel, nmp), in_specs=[pl.BlockS...  71.1 us
    pallas_call x1, Pallas kernels, fetch(): pl.pallas_call(functools.partial(fetch_kernel, nmp), in_specs=[vmem()] *...  39.7 us
    pallas_call x1, Pallas kernels, spread(): pl.pallas_call(spread_kernel, in_specs=[pl.BlockSpec(memory_space=pltpu.S...  30.5 us
    pallas_call x1, Pallas kernels, attend(): pl.pallas_call(attend_kernel, grid=(heads,), in_specs=[feat, feat, cells,...  9.13 us

profile of v2, /device:TPU:1, one launch (start us, length us, event | category | flops | bytes accessed | tf_op | source)
XLA Modules:
  0.0 171.1 jit_solution(7082721756062161352)
XLA Ops:
  0.6 0.0 copy-start
  2.0 0.7 fusion.3
  2.7 0.7 pad_add_fusion
  3.4 0.1 multiply_add_fusion
  3.5 0.1 add.100
  3.6 0.1 compare_reduce_fusion
  3.7 0.6 broadcast_in_dim.32.info_ref
  4.3 0.1 broadcast_in_dim.36
  4.3 0.1 concatenate.26
  4.4 0.8 pad_maximum_fusion
  5.3 0.8 copy.34
  6.0 39.7 %fetch.1 = (bf16[16,8,16,384]{3,2,1,0:T(8,128)(2,1)}, s32[8,8,128]{2,1,0:T(8,128)}, bf16[4,192,128]{2,1,0:T(8,128)(2,1)}, bf16[8,16,384]{2,1,0:T(8,128)(2,1)}, s32[8,128]{1,0:T(8,128)}) custom-call(bf16[8,16,384]{2,1,0:T(8,128)(2,1)} %bitcast.46, s32[8,128]{1,0:T(8,128)} %broadcast_in_dim.32.info_ref, bf16[192,128]{1,0:T(8,128)(2,1)} %cot_ref.1), custom_call_target="tpu_custom_call" | custom-call | tf_op jit(solution)/shard_map/fetch/pallas_call | solution.py:182
  45.7 1.3 slice.16
  47.0 0.7 compare_bitcast_fusion
  47.7 0.8 and_select_fusion.1
  48.5 0.9 select_reduce_fusion.index_ref
  49.4 0.0 copy-start.1
  49.4 30.5 %spread.1 = bf16[8,16,16,384]{3,2,1,0:T(8,128)(2,1)} custom-call(s32[8,16]{1,0:T(8,128)} %select_reduce_fusion.index_ref, bf16[16,8,16,384]{3,2,1,0:T(8,128)(2,1)} %get-tuple-element.21.table_ref), custom_call_target="tpu_custom_call" | custom-call | tf_op jit(solution)/shard_map/spread/pallas_call | solution.py:216
  79.9 0.0 copy-done
  79.9 0.0 copy-done.1
  79.9 0.8 fusion.1.da_ref
  80.8 1.4 copy.35.seen_ref
  82.2 9.1 %attend.1 = (bf16[192,128]{1,0:T(8,128)(2,1)}, bf16[192,128]{1,0:T(8,128)(2,1)}, bf16[128,384]{1,0:T(8,128)(2,1)}, f32[128,384]{1,0:T(8,128)}, bf16[2048,384]{1,0:T(8,128)(2,1)}) custom-call(bf16[192,128]{1,0:T(8,128)(2,1)} %q_ref.1, bf16[192,128]{1,0:T(8,128)(2,1)} %fusion.1.da_ref, bf16[128,384]{1,0:T(8,128)(2,1)} %bitcast.54, bf16[128,384]{1,0:T(8,128)(2,1)} %bitcast.47, ...), custom_call_target="tpu_custom_call" | custom-call | tf_op jit(solution)/shard_map/attend/pallas_call | solution.py:58
  91.3 1.0 convolution_convert_fusion
  92.4 1.0 fusion
  93.4 0.8 copy.36
  94.2 0.3 reshape.165
  94.5 0.9 pad.4.weight_ref
  95.4 71.1 %settle.1 = (bf16[8,16,384]{2,1,0:T(8,128)(2,1)}, bf16[192,128]{1,0:T(8,128)(2,1)}, f32[8,16,16,128]{3,2,1,0:T(8,128)}) custom-call(s32[8,16]{1,0:T(8,128)} %select_reduce_fusion.index_ref, bf16[8,16,16,384]{3,2,1,0:T(8,128)(2,1)} %bitcast.44, bf16[8,16,384]{2,1,0:T(8,128)(2,1)} %bitcast.55, f32[8,16,384]{2,1,0:T(8,128)} %bitcast.53, ...), custom_call_target="tpu_custom_call" | custom-call | tf_op jit(solution)/shard_map/settle/pallas_call | solution.py:358
  166.6 0.0 copy-start.2
  166.6 1.0 copy.37
  167.6 0.6 fusion.4
  168.2 2.2 %reshape.168 = f32[192,768]{1,0:T(8,128)} reshape(f32[8,16,9,128]{3,2,1,0:T(8,128)} %bitcast.45) | data formatting | bytes 1179648 | tf_op jit(solution)/shard_map/reshape | solution.py:432
  170.5 0.0 copy-done.2
  170.5 0.6 copy.41
  (5 shorter events, 0.0 us)
Async XLA Ops:
  0.6 79.3 %copy-start = (bf16[192,768]{1,0:T(8,128)(2,1)S(1)}, bf16[192,768]{1,0:T(8,128)(2,1)}, u32[]{:S(2)}) copy-start(bf16[192,768]{1,0:T(8,128)(2,1)} %param.11) | copy-start | bytes 884740
  49.4 30.5 %copy-start.1 = (bf16[4,192,128]{2,1,0:T(8,128)(2,1)S(1)}, bf16[4,192,128]{2,1,0:T(8,128)(2,1)}, u32[]{:S(2)}) copy-start(bf16[4,192,128]{2,1,0:T(8,128)(2,1)} %get-tuple-element.19) | copy-start | bytes 589828
  166.6 3.9 %copy-start.2 = (bf16[192,128]{1,0:T(8,128)(2,1)S(1)}, bf16[192,128]{1,0:T(8,128)(2,1)}, u32[]{:S(2)}) copy-start(bf16[192,128]{1,0:T(8,128)(2,1)} %get-tuple-element.44) | copy-start | bytes 147460

commit v3 on v2

--- a/solution.py
+++ b/solution.py
@@ -74,7 +74,7 @@
 MESH = pl.DeviceIdType.MESH
 HOPS = (NZ // 2, NZ - NZ // 2 - 1)
 HALF = ROWS_BLK // 2
-SPARE = 16
+LUMPS = 9
 
 
 def remote(source, target, sems, spot, device):
@@ -239,36 +239,46 @@
     mp_peers = [{"mp": step_round(mp, d, nmp)} for d in range(1, nmp)]
     peers = side_peers(side)
     meet(z_peers + peers + mp_peers + [after, before])
-    side_copies, w1, others = [], [], []
-    for d in FAR_FIRST:
-        to = step_round(side, d + 1, NSIDE)
-        side_copies.append(remote(slots_ref.at[to], parts.at[side], (side_send, side_recv), d, peers[d]))
-        w1.append(remote(weight_ref.at[to], wside.at[side], (w1_send, w1_recv), d, peers[d]))
+    side_copies, w1, others = {}, [], []
+    order = [spot for s in range(HOPS[0]) for spot in ((NZ // 2 - s), (NZ // 2 + 1 + s) % NZ)]
+    for turn, k in enumerate(order):
+        t = step_round(z, k, NZ)
+        if turn == 4:
+            for d in FAR_FIRST:
+                to = step_round(side, d + 1, NSIDE)
+                w1.append(remote(weight_ref.at[to], wside.at[side], (w1_send, w1_recv), d, peers[d]))
+                w1[-1].start()
+        for d in FAR_FIRST:
+            to = step_round(side, d + 1, NSIDE)
+            copy = remote(slots_ref.at[to, t], parts.at[side, t], (side_send, side_recv), (k, d), peers[d])
+            copy.start()
+            side_copies[k, d] = copy
     for d, peer in enumerate(mp_peers):
         to = step_round(mp, d + 1, nmp)
         others.append(remote(out_ref.at[to], mixes.at[mp], (mp_send, mp_recv), d, peer))
     others.append(remote(dprior_ref, back, (line_send, line_recv), 0, before))
-    for copy in side_copies + w1 + others:
+    for copy in others:
         copy.start()
     parts[side] = slots_ref[side]
     wside[side] = weight_ref[side]
     mixes[mp] = out_ref[mp]
-    for copy in side_copies:
-        copy.wait_recv()
-
-    def fill(t, carry):
+
+    def fill(k):
+        t = step_round(z, k, NZ)
+        for d in FAR_FIRST:
+            side_copies[k, d].wait_recv()
         for row in range(ROWS_BLK):
             total = jnp.zeros(parts.shape[2:], f32)
             for peer in range(NSIDE):
                 mark = jnp.where(index_ref[peer, t] == row, 1.0, 0.0)
                 total = total + parts[peer, t].astype(f32) * mark
             share[t, row] = total
-        return carry
-
-    lax.fori_loop(0, NZ, fill, 0)
+
     ring = {}
-    w2, w3, w4 = [], [], []
+    w4 = []
     for s in range(HOPS[0]):
+        for k in order[2 * s : 2 * s + 2]:
+            fill(k)
         for half in range(2):
             rows = pl.ds(half * HALF, HALF)
             for way in range(2):
@@ -285,7 +295,7 @@
                 )
                 copy.start()
                 ring[way, s, half] = copy
-        if s == 0:
+        if s == 2:
             for copy in w1:
                 copy.wait_recv()
             summed = wside[0].astype(f32)
@@ -294,23 +304,30 @@
             wsum[...] = summed.astype(bf)
             for d, peer in enumerate(z_peers):
                 to = step_round(z, d + 1, NZ)
-                w2.append(remote(wsum.at[to], wz.at[z], (w2_send, w2_recv), d, peer))
-                w2[-1].start()
-            wz[z] = wsum[z]
-        if s == 3:
-            for copy in w2:
-                copy.wait_recv()
-            one = wz[0].astype(f32)
-            for peer in range(1, NZ):
-                one = one + wz[peer].astype(f32)
-            wone[...] = one
+
+                @pl.when(to < LUMPS)
+                def _():
+                    remote(wsum.at[to], wz.at[z], (w2_send, w2_recv), d, peer).start()
+        if s == 4:
+
+            @pl.when(z < LUMPS)
+            def _():
+                for d, peer in enumerate(z_peers):
+                    remote(wsum.at[0], wz.at[z], (w2_send, w2_recv), d, peer).wait_recv()
+                wz[z] = wsum[z]
+                one = wz[0].astype(f32)
+                for peer in range(1, NZ):
+                    one = one + wz[peer].astype(f32)
+                wone[...] = one.astype(bf)
+                for d, peer in enumerate(z_peers):
+                    remote(wone, wring.at[z], (w3_send, w3_recv), d, peer).start()
+                wring[z] = wone[...]
+        if s == 7:
             for d, peer in enumerate(z_peers):
-                w3.append(remote(wone, wring.at[z], (w3_send, w3_recv), d, peer))
-                w3[-1].start()
-            wring[z] = wone[...]
-        if s == 6:
-            for copy in w3:
-                copy.wait_recv()
+
+                @pl.when(step_round(z, -d - 1, NZ) < LUMPS)
+                def _():
+                    remote(wone, wring.at[0], (w3_send, w3_recv), d, peer).wait_recv()
             for d in FAR_FIRST:
                 w4.append(remote(wring, wall_ref.at[side], (w4_send, w4_recv), d, peers[d]))
                 w4[-1].start()
@@ -330,8 +347,18 @@
     total_ref[...] = total.astype(bf)
     for copy in w4:
         copy.wait()
-    for copy in list(ring.values()) + side_copies + w1 + w2 + w3:
+    for copy in list(ring.values()) + list(side_copies.values()) + w1:
         copy.wait_send()
+    for d, peer in enumerate(z_peers):
+
+        @pl.when(step_round(z, d + 1, NZ) < LUMPS)
+        def _():
+            remote(wsum.at[0], wz.at[z], (w2_send, w2_recv), d, peer).wait_send()
+
+    @pl.when(z < LUMPS)
+    def _():
+        for d, peer in enumerate(z_peers):
+            remote(wone, wring.at[0], (w3_send, w3_recv), d, peer).wait_send()
 
 
 def settle(index, slots, dprior, down, out, weight):
@@ -349,11 +376,11 @@
         (out.shape, bf),
         (weight.shape, bf),
         (piece, bf),
+        ((NZ,) + piece[1:], bf),
+        (piece[1:], bf),
         (piece, bf),
-        (piece[1:], f32),
-        (piece, f32),
     ]
-    sems = pair_sems(2, HOPS[0], 2) + pair_sems(NSIDE - 1) + pair_sems(nmp - 1) + pair_sems(1)
+    sems = pair_sems(2, HOPS[0], 2) + pair_sems(NZ, NSIDE - 1) + pair_sems(nmp - 1) + pair_sems(1)
     sems += pair_sems(NSIDE - 1) + pair_sems(NZ - 1) + pair_sems(NZ - 1) + pair_sems(NSIDE - 1)
     return pl.pallas_call(
         functools.partial(settle_kernel, nmp),
@@ -362,7 +389,7 @@
         out_shape=[
             jax.ShapeDtypeStruct(block, bf),
             jax.ShapeDtypeStruct(out.shape[1:], bf),
-            jax.ShapeDtypeStruct(weight.shape, f32),
+            jax.ShapeDtypeStruct(weight.shape, bf),
         ],
         scratch_shapes=[pltpu.VMEM(*shape) for shape in scratch] + sems,
         compiler_params=pltpu.CompilerParams(collective_id=2, has_side_effects=True),
@@ -414,9 +441,9 @@
     weight_part = lax.dot_general(
         attended, cotangent_all, (((1,), (1,)), ((), ())), preferred_element_type=f32
     )
-    pieces = weight_part.astype(bf).reshape(NSIDE, NZ, -1, 128)
-    used = pieces.shape[2]
-    pieces = jnp.pad(pieces, ((0, 0), (0, 0), (0, SPARE - used), (0, 0)))
+    high, wide = features // ROW_CELLS, weight_part.shape[1] // 128
+    pieces = weight_part.astype(bf).reshape(high, ROW_CELLS, wide, 128).transpose(0, 2, 1, 3)
+    pieces = pieces.reshape(NSIDE, LUMPS, ROW_CELLS, 128)
     partial_out = lax.dot_general(
         out_weight, attended, (((0,), (0,)), ((), ())), preferred_element_type=f32
     )
@@ -429,7 +456,8 @@
         partial_out.astype(bf).reshape(nmp, features, CELLS_BLK),
         pieces,
     )
-    weight_grad = weight_all[:, :, :used].reshape(features, -1)
+    weight_grad = weight_all.reshape(high, wide, ROW_CELLS, 128).transpose(0, 2, 1, 3)
+    weight_grad = weight_grad.reshape(features, -1).astype(f32)
     d_pairs = total.reshape(CELLS_BLK, width).T.reshape(heads, 2, HEAD_DIM, CELLS_BLK)
     d_key_cells = d_pairs[:, 0].reshape(features, CELLS_BLK)
     d_value_cells = d_pairs[:, 1].reshape(features, CELLS_BLK)

time: 172 us -> 152 us (0.88)
  Pallas kernels: 150 us -> 132 us
    pallas_call x1, Pallas kernels: 71.1 us -> 52.1 us  [settle(): pl.pallas_call(functools.partial(settle_kernel, nmp), in_specs=[pl.BlockS...]
    reshape x2 -> x1, local copies, waits for them, and re-layouts: 2.5 us -> 0.35 us  [on_device(): weight_part.astype(bf).reshape(high, ROW_CELLS, wide, 128)]
where the time goes in v3:
time: 152 us; the launch traced here: 151 us
  Pallas kernels  132 us (87%)
  local copies, waits for them, and re-layouts  10.5 us (7%)
  other arithmetic  4.74 us (3%)
  matrix products  2.17 us (1%)
  between operations  2.12 us (1%)
    pallas_call x1, Pallas kernels, settle(): pl.pallas_call(functools.partial(settle_kernel, nmp), in_specs=[pl.BlockS...  52.1 us
    pallas_call x1, Pallas kernels, fetch(): pl.pallas_call(functools.partial(fetch_kernel, nmp), in_specs=[vmem()] *...  39.7 us
    pallas_call x1, Pallas kernels, spread(): pl.pallas_call(spread_kernel, in_specs=[pl.BlockSpec(memory_space=pltpu.S...  30.5 us
    pallas_call x1, Pallas kernels, attend(): pl.pallas_call(attend_kernel, grid=(heads,), in_specs=[feat, feat, cells,...  9.14 us

profile of v3, /device:TPU:1, one launch (start us, length us, event | category | flops | bytes accessed | tf_op | source)
XLA Modules:
  0.0 151.0 jit_solution(16462939970822687002)
XLA Ops:
  0.6 0.0 copy-start
  2.0 0.7 fusion.3
  2.7 0.7 pad_add_fusion
  3.4 0.1 multiply_add_fusion
  3.5 0.1 add.98
  3.6 0.1 compare_reduce_fusion
  3.7 0.6 broadcast_in_dim.32.info_ref
  4.3 0.1 broadcast_in_dim.36
  4.3 0.1 concatenate.26
  4.4 0.8 pad_maximum_fusion
  5.3 0.8 copy.42
  6.0 39.7 %fetch.1 = (bf16[16,8,16,384]{3,2,1,0:T(8,128)(2,1)}, s32[8,8,128]{2,1,0:T(8,128)}, bf16[4,192,128]{2,1,0:T(8,128)(2,1)}, bf16[8,16,384]{2,1,0:T(8,128)(2,1)}, s32[8,128]{1,0:T(8,128)}) custom-call(bf16[8,16,384]{2,1,0:T(8,128)(2,1)} %bitcast.57, s32[8,128]{1,0:T(8,128)} %broadcast_in_dim.32.info_ref, bf16[192,128]{1,0:T(8,128)(2,1)} %cot_ref.1), custom_call_target="tpu_custom_call" | custom-call | tf_op jit(solution)/shard_map/fetch/pallas_call | solution.py:182
  45.7 1.3 slice.13
  47.0 0.7 compare_bitcast_fusion
  47.7 0.8 and_select_fusion.1
  48.5 0.9 select_reduce_fusion.index_ref
  49.4 0.0 copy-start.1
  49.4 30.5 %spread.1 = bf16[8,16,16,384]{3,2,1,0:T(8,128)(2,1)} custom-call(s32[8,16]{1,0:T(8,128)} %select_reduce_fusion.index_ref, bf16[16,8,16,384]{3,2,1,0:T(8,128)(2,1)} %get-tuple-element.21.table_ref), custom_call_target="tpu_custom_call" | custom-call | tf_op jit(solution)/shard_map/spread/pallas_call | solution.py:216
  79.9 0.0 copy-done
  79.9 0.0 copy-done.1
  79.9 0.8 fusion.1.da_ref
  80.8 1.4 copy.43.seen_ref
  82.2 9.1 %attend.1 = (bf16[192,128]{1,0:T(8,128)(2,1)}, bf16[192,128]{1,0:T(8,128)(2,1)}, bf16[128,384]{1,0:T(8,128)(2,1)}, f32[128,384]{1,0:T(8,128)}, bf16[2048,384]{1,0:T(8,128)(2,1)}) custom-call(bf16[192,128]{1,0:T(8,128)(2,1)} %q_ref.1, bf16[192,128]{1,0:T(8,128)(2,1)} %fusion.1.da_ref, bf16[128,384]{1,0:T(8,128)(2,1)} %bitcast.67, bf16[128,384]{1,0:T(8,128)(2,1)} %bitcast.58, ...), custom_call_target="tpu_custom_call" | custom-call | tf_op jit(solution)/shard_map/attend/pallas_call | solution.py:58
  91.3 0.0 copy-start.2
  91.4 1.1 convolution_convert_fusion
  92.5 0.3 reshape.171
  92.8 0.8 copy.45
  93.6 0.0 copy-done.2
  93.6 0.2 fusion
  93.8 0.8 copy.44
  94.6 52.1 %settle.1 = (bf16[8,16,384]{2,1,0:T(8,128)(2,1)}, bf16[192,128]{1,0:T(8,128)(2,1)}, bf16[8,9,16,128]{3,2,1,0:T(8,128)(2,1)}) custom-call(s32[8,16]{1,0:T(8,128)} %select_reduce_fusion.index_ref, bf16[8,16,16,384]{3,2,1,0:T(8,128)(2,1)} %bitcast.54, bf16[8,16,384]{2,1,0:T(8,128)(2,1)} %bitcast.68, f32[8,16,384]{2,1,0:T(8,128)} %bitcast.66, ...), custom_call_target="tpu_custom_call" | custom-call | tf_op jit(solution)/shard_map/settle/pallas_call | solution.py:385
  146.8 0.0 copy-start.3
  146.8 1.0 copy.46
  147.8 0.6 fusion.4
  148.4 1.0 copy.47
  149.5 0.9 copy.50
  150.4 0.0 copy-done.3
  150.4 0.6 copy.54
  (5 shorter events, 0.0 us)
Async XLA Ops:
  0.6 79.3 %copy-start = (bf16[192,768]{1,0:T(8,128)(2,1)S(1)}, bf16[192,768]{1,0:T(8,128)(2,1)}, u32[]{:S(2)}) copy-start(bf16[192,768]{1,0:T(8,128)(2,1)} %param.11) | copy-start | bytes 884740
  49.4 30.5 %copy-start.1 = (bf16[4,192,128]{2,1,0:T(8,128)(2,1)S(1)}, bf16[4,192,128]{2,1,0:T(8,128)(2,1)}, u32[]{:S(2)}) copy-start(bf16[4,192,128]{2,1,0:T(8,128)(2,1)} %get-tuple-element.19) | copy-start | bytes 589828
  91.3 2.2 %copy-start.2 = (bf16[192,128]{1,0:T(8,128)(2,1)S(1)}, bf16[192,128]{1,0:T(8,128)(2,1)}, u32[]{:S(2)}) copy-start(bf16[192,128]{1,0:T(8,128)(2,1)} %get-tuple-element.26) | copy-start | bytes 147460
  146.8 3.7 %copy-start.3 = (bf16[192,128]{1,0:T(8,128)(2,1)S(1)}, bf16[192,128]{1,0:T(8,128)(2,1)}, u32[]{:S(2)}) copy-start(bf16[192,128]{1,0:T(8,128)(2,1)} %get-tuple-element.44) | copy-start | bytes 147460

commit v4 on v3

--- a/solution.py
+++ b/solution.py
@@ -112,53 +112,91 @@
     return [side_device(step_round(side, d, NSIDE)) for d in range(1, NSIDE)]
 
 
+FAR_FIRST = (3, 2, 4, 1, 5, 0, 6)
+
+
 def fetch_kernel(
-    nmp, own_ref, info_ref, cot_ref, table_ref, asked_ref, cots_ref, prior_ref, told_ref,
-    ring_send, ring_recv, side_send, side_recv, mp_send, mp_recv, line_send, line_recv,
+    nmp, fanout, own_ref, info_ref, cot_ref, slots_ref, index_ref, cots_ref, prior_ref, told_ref,
+    table, asked, held, ready, spots,
+    ring_send, ring_recv, info_send, info_recv, side_send, side_recv, mp_send, mp_recv, line_send, line_recv, spots_sem,
 ):
     x, z, c, mp = (lax.axis_index(name) for name in ROW + ("mp",))
     side = x * NC + c
     ways = [{"z": step_round(z, 1, NZ)}, {"z": step_round(z, -1, NZ)}]
     after, before = line_device(x, z, c, 1), line_device(x, z, c, -1)
     mp_peers = [{"mp": step_round(mp, d, nmp)} for d in range(1, nmp)]
-    meet(ways + side_peers(side) + mp_peers + [after, before])
-    ring = {}
+    peers = side_peers(side)
+    meet(ways + peers + mp_peers + [after, before])
+    ring, picked = {}, {}
 
     def hop(way, s, half):
         rows = pl.ds(half * HALF, HALF)
         block = step_round(z, s if way else -s, NZ)
-        source = table_ref.at[block, rows] if s else own_ref.at[rows]
-        copy = remote(source, table_ref.at[block, rows], (ring_send, ring_recv), (way, s, half), ways[way])
+        source = table.at[block, rows] if s else own_ref.at[rows]
+        copy = remote(source, table.at[block, rows], (ring_send, ring_recv), (way, s, half), ways[way])
         copy.start()
         ring[way, s, half] = copy
 
+    def pick(distance):
+        block, k = step_round(z, distance, NZ), distance % NZ
+        ready[...] = table[block]
+        for d in FAR_FIRST:
+            to = step_round(side, d + 1, NSIDE)
+            held[d, block] = ready[spots[block, to]]
+            copy = remote(held.at[d, block], slots_ref.at[side, block], (side_send, side_recv), (k, d), peers[d])
+            copy.start()
+            picked[k, d] = copy
+        slots_ref[side, block] = ready[spots[block, side]]
+
+    infos = [remote(info_ref, asked.at[side], (info_send, info_recv), d, peers[d]) for d in FAR_FIRST]
+    for copy in infos:
+        copy.start()
     for half in range(2):
         for way in range(2):
             hop(way, 0, half)
     others = []
-    for d, peer in enumerate(side_peers(side)):
-        others.append(remote(info_ref, asked_ref.at[side], (side_send, side_recv), d, peer))
     for d, peer in enumerate(mp_peers):
         others.append(remote(cot_ref, cots_ref.at[mp], (mp_send, mp_recv), d, peer))
-    others.append(remote(own_ref, prior_ref, (line_send, line_recv), 0, after))
-    others.append(remote(info_ref, told_ref, (line_send, line_recv), 1, after))
-    for copy in others:
-        copy.start()
-    table_ref[z] = own_ref[...]
-    asked_ref[side] = info_ref[...]
+        others[-1].start()
+    table[z] = own_ref[...]
+    asked[side] = info_ref[...]
     cots_ref[mp] = cot_ref[...]
-    for s in range(1, HOPS[0]):
+    for copy in infos:
+        copy.wait_recv()
+    shape = (NZ, 128)
+    owner = (x * NZ + lax.broadcasted_iota(jnp.int32, shape, 0)) * NC + c
+    lane = lax.broadcasted_iota(jnp.int32, shape, 1)
+    found = jnp.zeros(shape, jnp.int32)
+    for peer in range(NSIDE):
+        wanted = jnp.concatenate([asked[peer]] * (NZ // 8), axis=0)
+        hit = (lax.shift_right_logical(wanted, 3) == owner) & (lane < fanout)
+        local = jnp.sum(jnp.where(hit, wanted & 7, 0), axis=1, keepdims=True)
+        found = jnp.where(lane == peer, local, found)
+    index_ref[...] = found
+    local_copy = pltpu.make_async_copy(index_ref, spots, spots_sem.at[0])
+    local_copy.start()
+    local_copy.wait()
+    pick(0)
+    for s in range(1, HOPS[0] + 1):
         for half in range(2):
             for way in range(2):
+                if s <= HOPS[way]:
+                    ring[way, s - 1, half].wait_recv()
                 if s < HOPS[way]:
-                    ring[way, s - 1, half].wait_recv()
                     hop(way, s, half)
-    for half in range(2):
+        if s == 5:
+            others.append(remote(own_ref, prior_ref, (line_send, line_recv), 0, after))
+            others.append(remote(info_ref, told_ref, (line_send, line_recv), 1, after))
+            for copy in others[-2:]:
+                copy.start()
         for way in range(2):
-            ring[way, HOPS[way] - 1, half].wait_recv()
+            if s <= HOPS[way]:
+                pick(s if way else -s)
     for copy in others:
         copy.wait()
-    for copy in ring.values():
+    for copy in picked.values():
+        copy.wait()
+    for copy in list(ring.values()) + infos:
         copy.wait_send()
 
 
@@ -170,58 +208,34 @@
     return [pltpu.SemaphoreType.DMA(shape), pltpu.SemaphoreType.DMA(shape)]
 
 
-def fetch(own, info, cot, nmp):
+def fetch(own, info, cot, nmp, fanout):
     bf, i32 = jnp.bfloat16, jnp.int32
+    tail = own.shape[1:]
     shapes = [
-        ((NZ,) + own.shape, bf),
-        ((NSIDE,) + info.shape, i32),
+        ((NSIDE, NZ) + tail, bf),
+        ((NZ, 128), i32),
         ((nmp,) + cot.shape, bf),
         (own.shape, bf),
         (info.shape, i32),
     ]
+    scratch = [
+        pltpu.VMEM((NZ,) + own.shape, bf),
+        pltpu.VMEM((NSIDE,) + info.shape, i32),
+        pltpu.VMEM((NSIDE - 1, NZ) + tail, bf),
+        pltpu.VMEM(own.shape, bf),
+        pltpu.SMEM((NZ, 128), i32),
+    ]
+    sems = pair_sems(2, HOPS[0], 2) + pair_sems(NSIDE - 1) + pair_sems(NZ, NSIDE - 1)
+    sems += pair_sems(nmp - 1) + pair_sems(2) + [pltpu.SemaphoreType.DMA((1,))]
     return pl.pallas_call(
-        functools.partial(fetch_kernel, nmp),
+        functools.partial(fetch_kernel, nmp, fanout),
         in_specs=[vmem()] * 3,
         out_specs=[vmem()] * 5,
         out_shape=[jax.ShapeDtypeStruct(*shape) for shape in shapes],
-        scratch_shapes=pair_sems(2, HOPS[0], 2) + pair_sems(NSIDE - 1) + pair_sems(nmp - 1) + pair_sems(2),
+        scratch_shapes=scratch + sems,
         compiler_params=pltpu.CompilerParams(collective_id=0, has_side_effects=True),
         name="fetch",
     )(own, info, cot)
-
-
-def spread_kernel(index_ref, table_ref, slots_ref, held, side_send, side_recv):
-    side = lax.axis_index("x") * NC + lax.axis_index("c")
-    peers = side_peers(side)
-    meet(peers)
-    copies = []
-    for d in FAR_FIRST:
-        to = step_round(side, d + 1, NSIDE)
-        for z in range(NZ):
-            held[d, z] = table_ref[z, index_ref[to, z]]
-        copy = remote(held.at[d], slots_ref.at[side], (side_send, side_recv), d, peers[d])
-        copy.start()
-        copies.append(copy)
-    for z in range(NZ):
-        slots_ref[side, z] = table_ref[z, index_ref[side, z]]
-    for copy in copies:
-        copy.wait()
-
-
-FAR_FIRST = (3, 2, 4, 1, 5, 0, 6)
-
-
-def spread(index, table):
-    tail = table.shape[2:]
-    return pl.pallas_call(
-        spread_kernel,
-        in_specs=[pl.BlockSpec(memory_space=pltpu.SMEM), vmem()],
-        out_specs=vmem(),
-        out_shape=jax.ShapeDtypeStruct((NSIDE, NZ) + tail, table.dtype),
-        scratch_shapes=[pltpu.VMEM((NSIDE - 1, NZ) + tail, table.dtype)] + pair_sems(NSIDE - 1),
-        compiler_params=pltpu.CompilerParams(collective_id=1, has_side_effects=True),
-        name="spread",
-    )(index, table)
 
 
 def settle_kernel(
@@ -270,7 +284,7 @@
         for row in range(ROWS_BLK):
             total = jnp.zeros(parts.shape[2:], f32)
             for peer in range(NSIDE):
-                mark = jnp.where(index_ref[peer, t] == row, 1.0, 0.0)
+                mark = jnp.where(index_ref[t, peer] == row, 1.0, 0.0)
                 total = total + parts[peer, t].astype(f32) * mark
             share[t, row] = total
 
@@ -392,7 +406,7 @@
             jax.ShapeDtypeStruct(weight.shape, bf),
         ],
         scratch_shapes=[pltpu.VMEM(*shape) for shape in scratch] + sems,
-        compiler_params=pltpu.CompilerParams(collective_id=2, has_side_effects=True),
+        compiler_params=pltpu.CompilerParams(collective_id=1, has_side_effects=True),
         name="settle",
     )(index, slots, dprior, down, out, weight)
 
@@ -415,16 +429,12 @@
     wanted = parent_rows.reshape(-1)
     lanes = jnp.concatenate([wanted, valid_cells, jnp.zeros(127 - wanted.shape[0], jnp.int32)])
     info = jnp.broadcast_to(lanes, (8, 128))
-    table, asked, cotangents, prior, told = fetch(
-        own.reshape(ROWS_BLK, ROW_CELLS, width), info, out_cotangent, nmp
+    slots, index, cotangents, prior, told = fetch(
+        own.reshape(ROWS_BLK, ROW_CELLS, width), info, out_cotangent, nmp, wanted.shape[0]
     )
     cotangent_all = cotangents.reshape(-1, CELLS_BLK)
     prior = prior.reshape(CELLS_BLK, width)
     prior_valid = told[0, wanted.shape[0]]
-    asked = asked[:, 0, : wanted.shape[0]]
-    owner_here = (x_at * NZ + jnp.arange(NZ)) * NC + c_at
-    hit = (asked // ROWS_BLK)[:, None, :] == owner_here[None, :, None]
-    index = jnp.sum(jnp.where(hit, (asked % ROWS_BLK)[:, None, :], 0), axis=-1)
     side_ids = jnp.arange(NSIDE)
     slot_owner = ((side_ids // NC)[:, None] * NZ + jnp.arange(NZ)[None, :]) * NC + (side_ids % NC)[:, None]
     slot_seen = jnp.any(slot_owner.reshape(-1)[:, None] == (wanted // ROWS_BLK)[None, :], axis=-1)
@@ -433,7 +443,6 @@
     seen = jnp.concatenate([prior_seen, cell_ids < valid, jnp.repeat(slot_seen, ROW_CELLS)])
     seen = seen.astype(f32)[:, None]
 
-    slots = spread(index, table)
     d_attended = jnp.dot(out_weight, cotangent_all, preferred_element_type=f32).astype(bf)
     attended, d_queries, d_prior, d_own, d_slots = attend(
         queries, d_attended, prior, own, slots.reshape(SLOTS * ROW_CELLS, width), seen

time: 152 us -> 132 us (0.87)
  Pallas kernels: 132 us -> 113 us
  other arithmetic: 4.74 us -> 3.07 us
    pallas_call x2 -> x1, Pallas kernels: 70.2 us -> 52.1 us  [fetch(): pl.pallas_call(functools.partial(fetch_kernel, nmp, fanout), in_specs=[vm...]
where the time goes in v4:
time: 132 us
  Pallas kernels  113 us (86%)
  local copies, waits for them, and re-layouts  10.5 us (8%)
  matrix products  3.09 us (2%)
  other arithmetic  3.07 us (2%)
  between operations  2.09 us (2%)
    pallas_call x1, Pallas kernels, fetch(): pl.pallas_call(functools.partial(fetch_kernel, nmp, fanout), in_specs=[vm...  52.1 us
    pallas_call x1, Pallas kernels, settle(): pl.pallas_call(functools.partial(settle_kernel, nmp), in_specs=[pl.BlockS...  51.9 us
    pallas_call x1, Pallas kernels, attend(): pl.pallas_call(attend_kernel, grid=(heads,), in_specs=[feat, feat, cells,...  9.18 us

profile of v4, /device:TPU:1, one launch (start us, length us, event | category | flops | bytes accessed | tf_op | source)
XLA Modules:
  0.0 132.0 jit_solution(2911142353127773789)
XLA Ops:
  0.6 0.0 copy-start
  2.0 0.7 fusion.3
  2.7 0.7 pad_add_fusion
  3.4 0.1 multiply_add_fusion
  3.5 0.1 add.64
  3.6 0.1 compare_reduce_fusion
  3.6 0.6 broadcast_in_dim.7.info_ref
  4.2 0.1 broadcast_in_dim.16
  4.3 0.1 concatenate.26
  4.4 0.8 pad_maximum_fusion
  5.3 0.8 copy.42
  6.0 52.1 %fetch.1 = (bf16[8,16,16,384]{3,2,1,0:T(8,128)(2,1)}, s32[16,128]{1,0:T(8,128)}, bf16[4,192,128]{2,1,0:T(8,128)(2,1)}, bf16[8,16,384]{2,1,0:T(8,128)(2,1)}, s32[8,128]{1,0:T(8,128)}) custom-call(bf16[8,16,384]{2,1,0:T(8,128)(2,1)} %bitcast.55, s32[8,128]{1,0:T(8,128)} %broadcast_in_dim.7.info_ref, bf16[192,128]{1,0:T(8,128)(2,1)} %cot_ref.1), custom_call_target="tpu_custom_call" | custom-call | tf_op jit(solution)/shard_map/fetch/pallas_call | solution.py:230
  58.1 1.3 slice.9
  59.4 0.7 compare_bitcast_fusion
  60.1 0.0 copy-done
  60.1 1.8 %fusion.1.da_ref = bf16[192,128]{1,0:T(8,128)(2,1)} fusion(bf16[192,768]{1,0:T(8,128)(2,1)S(1)} %copy-done, bf16[768,128]{1,0:T(8,128)(2,1)} %bitcast.58), kind=kOutput, calls=%fused_computation.4 | convolution fusion | flops 37773312 | bytes 540672 | tf_op jit(solution)/shard_map/dot_general | solution.py:446
  61.9 1.5 %copy.43.seen_ref = f32[2304,1]{1,0:T(8,128)} copy(f32[2304,1]{0,1:T(1,128)S(1)} %add_convert_fusion) | data formatting | bytes 18432 | tf_op jit(solution)/shard_map/convert_element_type | solution.py:444
  63.3 0.0 copy-start.1
  63.3 9.2 %attend.1 = (bf16[192,128]{1,0:T(8,128)(2,1)}, bf16[192,128]{1,0:T(8,128)(2,1)}, bf16[128,384]{1,0:T(8,128)(2,1)}, f32[128,384]{1,0:T(8,128)}, bf16[2048,384]{1,0:T(8,128)(2,1)}) custom-call(bf16[192,128]{1,0:T(8,128)(2,1)} %q_ref.1, bf16[192,128]{1,0:T(8,128)(2,1)} %fusion.1.da_ref, bf16[128,384]{1,0:T(8,128)(2,1)} %bitcast.65, bf16[128,384]{1,0:T(8,128)(2,1)} %bitcast.56, ...), custom_call_target="tpu_custom_call" | custom-call | tf_op jit(solution)/shard_map/attend/pallas_call | solution.py:58
  72.5 0.0 copy-start.2
  72.5 0.0 copy-done.1
  72.5 1.1 convolution_convert_fusion
  73.6 0.3 reshape.165
  74.0 0.8 copy.45
  74.7 0.0 copy-done.2
  74.7 0.2 fusion
  75.0 0.8 copy.44
  75.8 51.9 %settle.1 = (bf16[8,16,384]{2,1,0:T(8,128)(2,1)}, bf16[192,128]{1,0:T(8,128)(2,1)}, bf16[8,9,16,128]{3,2,1,0:T(8,128)(2,1)}) custom-call(s32[16,128]{1,0:T(8,128)} %get-tuple-element.18.index_ref, bf16[8,16,16,384]{3,2,1,0:T(8,128)(2,1)} %bitcast.52, bf16[8,16,384]{2,1,0:T(8,128)(2,1)} %bitcast.66, f32[8,16,384]{2,1,0:T(8,128)} %bitcast.64, ...), custom_call_target="tpu_custom_call" | custom-call | tf_op jit(solution)/shard_map/settle/pallas_call | solution.py:399
  127.7 0.0 copy-start.3
  127.7 1.0 copy.46
  128.7 0.6 fusion.4
  129.4 1.0 copy.47
  130.4 0.9 copy.50
  131.3 0.0 copy-done.3
  131.3 0.6 copy.54
  (3 shorter events, 0.0 us)
Async XLA Ops:
  0.6 59.5 %copy-start = (bf16[192,768]{1,0:T(8,128)(2,1)S(1)}, bf16[192,768]{1,0:T(8,128)(2,1)}, u32[]{:S(2)}) copy-start(bf16[192,768]{1,0:T(8,128)(2,1)} %param.11) | copy-start | bytes 884740
  63.3 9.2 %copy-start.1 = (bf16[4,192,128]{2,1,0:T(8,128)(2,1)S(1)}, bf16[4,192,128]{2,1,0:T(8,128)(2,1)}, u32[]{:S(2)}) copy-start(bf16[4,192,128]{2,1,0:T(8,128)(2,1)} %get-tuple-element.19) | copy-start | bytes 589828
  72.5 2.2 %copy-start.2 = (bf16[192,128]{1,0:T(8,128)(2,1)S(1)}, bf16[192,128]{1,0:T(8,128)(2,1)}, u32[]{:S(2)}) copy-start(bf16[192,128]{1,0:T(8,128)(2,1)} %get-tuple-element.26) | copy-start | bytes 147460
  127.7 3.7 %copy-start.3 = (bf16[192,128]{1,0:T(8,128)(2,1)S(1)}, bf16[192,128]{1,0:T(8,128)(2,1)}, u32[]{:S(2)}) copy-start(bf16[192,128]{1,0:T(8,128)(2,1)} %get-tuple-element.42) | copy-start | bytes 147460

commit v5 on v4

--- a/solution.py
+++ b/solution.py
@@ -18,18 +18,13 @@
 KEYS = 2 * CELLS_BLK + SLOTS * ROW_CELLS
 
 
-def attend_kernel(
-    q_ref, da_ref, prior_ref, own_ref, slots_ref, seen_ref, att_ref, dq_ref, dprior_ref, down_ref, dslots_ref
-):
+def attend(q, da, kv, visible):
     scale = HEAD_DIM ** (-0.5)
-    kv = jnp.concatenate([prior_ref[...], own_ref[...], slots_ref[...]], axis=0)
-    q, da = q_ref[...], da_ref[...]
     blank = jnp.zeros_like(q)
     both = jnp.concatenate(
         [jnp.concatenate([q, blank], axis=1), jnp.concatenate([blank, da], axis=1)], axis=0
     )
     cross = jnp.dot(kv, both, preferred_element_type=jnp.float32)
-    visible = seen_ref[...] > 0.5
     scores = jnp.where(visible, cross[:, :CELLS_BLK] * scale, -1e30)
     top = jnp.max(scores, axis=0, keepdims=True)
     grown = jnp.where(visible, jnp.exp(scores - top), 0.0)
@@ -41,34 +36,7 @@
     pair = jnp.concatenate([d_scores, probs_low], axis=1)
     d_kv = lax.dot_general(pair, both, (((1,), (1,)), ((), ())), preferred_element_type=jnp.float32)
     mixed = lax.dot_general(kv, pair, (((0,), (0,)), ((), ())), preferred_element_type=jnp.float32)
-    dq_ref[...] = mixed[:HEAD_DIM, :CELLS_BLK].astype(jnp.bfloat16)
-    att_ref[...] = mixed[HEAD_DIM:, CELLS_BLK:].astype(jnp.bfloat16)
-    dprior_ref[...] = d_kv[:CELLS_BLK].astype(jnp.bfloat16)
-    down_ref[...] = d_kv[CELLS_BLK : 2 * CELLS_BLK]
-    dslots_ref[...] = d_kv[2 * CELLS_BLK :].astype(jnp.bfloat16)
-
-
-def attend(q, da, prior, own, slots, seen):
-    heads = q.shape[0] // HEAD_DIM
-    width = own.shape[1]
-    feat = pl.BlockSpec((HEAD_DIM, CELLS_BLK), lambda h: (h, 0))
-    cells = pl.BlockSpec((CELLS_BLK, 2 * HEAD_DIM), lambda h: (0, h))
-    many = pl.BlockSpec((SLOTS * ROW_CELLS, 2 * HEAD_DIM), lambda h: (0, h))
-    bf, f32 = jnp.bfloat16, jnp.float32
-    return pl.pallas_call(
-        attend_kernel,
-        grid=(heads,),
-        in_specs=[feat, feat, cells, cells, many, pl.BlockSpec((KEYS, 1), lambda h: (0, 0))],
-        out_specs=[feat, feat, cells, cells, many],
-        out_shape=[
-            jax.ShapeDtypeStruct(q.shape, bf),
-            jax.ShapeDtypeStruct(q.shape, bf),
-            jax.ShapeDtypeStruct((CELLS_BLK, width), bf),
-            jax.ShapeDtypeStruct((CELLS_BLK, width), f32),
-            jax.ShapeDtypeStruct((SLOTS * ROW_CELLS, width), bf),
-        ],
-        name="attend",
-    )(q, da, prior, own, slots, seen)
+    return d_kv, mixed[:HEAD_DIM, :CELLS_BLK], mixed[HEAD_DIM:, CELLS_BLK:]
 
 
 MESH = pl.DeviceIdType.MESH
@@ -239,7 +207,9 @@
 
 
 def settle_kernel(
-    nmp, index_ref, slots_ref, dprior_ref, down_ref, out_ref, weight_ref, total_ref, mixed_ref, wall_ref,
+    nmp, index_ref, q_ref, da_ref, prior_ref, own_ref, keys_ref, seen_ref, proj_ref, cot_ref,
+    total_ref, mixed_ref, dq_ref, wall_ref,
+    slots_ref, dprior_ref, down_ref, att_ref, out_ref, weight_ref,
     parts, share, sent, got, back, mixes, wside, wsum, wz, wone, wring,
     ring_send, ring_recv, side_send, side_recv, mp_send, mp_recv, line_send, line_recv,
     w1_send, w1_recv, w2_send, w2_recv, w3_send, w3_recv, w4_send, w4_recv,
@@ -252,7 +222,32 @@
     after, before = line_device(x, z, c, 1), line_device(x, z, c, -1)
     mp_peers = [{"mp": step_round(mp, d, nmp)} for d in range(1, nmp)]
     peers = side_peers(side)
-    meet(z_peers + peers + mp_peers + [after, before])
+    everyone = z_peers + peers + mp_peers + [after, before]
+    barrier = pltpu.get_barrier_semaphore()
+    for peer in everyone:
+        pl.semaphore_signal(barrier, inc=1, device_id=peer, device_id_type=MESH)
+    visible = seen_ref[...] > 0.5
+    for head in range(q_ref.shape[0] // HEAD_DIM):
+        feats = slice(head * HEAD_DIM, (head + 1) * HEAD_DIM)
+        cols = slice(head * 2 * HEAD_DIM, (head + 1) * 2 * HEAD_DIM)
+        kv = jnp.concatenate([prior_ref[:, cols], own_ref[:, cols], keys_ref[:, cols]], axis=0)
+        d_kv, dq, att = attend(q_ref[feats, :], da_ref[feats, :], kv, visible)
+        dq_ref[feats, :] = dq.astype(bf)
+        att_ref[feats, :] = att.astype(bf)
+        block = (ROWS_BLK, ROW_CELLS, 2 * HEAD_DIM)
+        dprior_ref[:, :, cols] = d_kv[:CELLS_BLK].astype(bf).reshape(block)
+        down_ref[:, :, cols] = d_kv[CELLS_BLK : 2 * CELLS_BLK].reshape(block)
+        slots_ref[:, :, :, cols] = d_kv[2 * CELLS_BLK :].astype(bf).reshape((NSIDE, NZ) + block[1:])
+    attended = att_ref[...]
+    out = lax.dot_general(proj_ref[...], attended, (((0,), (0,)), ((), ())), preferred_element_type=f32)
+    out_ref[...] = out.astype(bf).reshape(out_ref.shape)
+    weight = lax.dot_general(attended, cot_ref[...], (((1,), (1,)), ((), ())), preferred_element_type=f32)
+    weight = weight.astype(bf)
+    wide = weight.shape[1] // 128
+    for tile in range(NSIDE * LUMPS):
+        row, col = tile // wide * ROW_CELLS, tile % wide * 128
+        weight_ref[tile // LUMPS, tile % LUMPS] = weight[row : row + ROW_CELLS, col : col + 128]
+    pl.semaphore_wait(barrier, len(everyone))
     side_copies, w1, others = {}, [], []
     order = [spot for s in range(HOPS[0]) for spot in ((NZ // 2 - s), (NZ // 2 + 1 + s) % NZ)]
     for turn, k in enumerate(order):
@@ -375,20 +370,30 @@
             remote(wone, wring.at[0], (w3_send, w3_recv), d, peer).wait_send()
 
 
-def settle(index, slots, dprior, down, out, weight):
+def settle(index, q, da, prior, own, keys, seen, proj, cot):
     bf, f32 = jnp.bfloat16, jnp.float32
-    nmp = out.shape[0]
-    tail = slots.shape[2:]
+    features, width = own.shape[1] // 2, own.shape[1]
+    nmp = cot.shape[0] // features
+    tail = (ROW_CELLS, width)
     block = (ROWS_BLK,) + tail
-    piece = weight.shape[1:]
+    slots = (NSIDE, NZ) + tail
+    outs = (nmp, features, CELLS_BLK)
+    pieces = (NSIDE, LUMPS, ROW_CELLS, 128)
+    piece = pieces[1:]
     scratch = [
-        (slots.shape, bf),
+        (slots, bf),
+        (block, bf),
+        (block, f32),
+        (q.shape, bf),
+        (outs, bf),
+        (pieces, bf),
+        (slots, bf),
         ((NZ,) + block, f32),
         ((2, HOPS[0]) + block, bf),
         ((2, HOPS[0]) + block, bf),
         (block, bf),
-        (out.shape, bf),
-        (weight.shape, bf),
+        (outs, bf),
+        (pieces, bf),
         (piece, bf),
         ((NZ,) + piece[1:], bf),
         (piece[1:], bf),
@@ -398,17 +403,18 @@
     sems += pair_sems(NSIDE - 1) + pair_sems(NZ - 1) + pair_sems(NZ - 1) + pair_sems(NSIDE - 1)
     return pl.pallas_call(
         functools.partial(settle_kernel, nmp),
-        in_specs=[pl.BlockSpec(memory_space=pltpu.SMEM)] + [vmem()] * 5,
-        out_specs=[vmem()] * 3,
+        in_specs=[pl.BlockSpec(memory_space=pltpu.SMEM)] + [vmem()] * 8,
+        out_specs=[vmem()] * 4,
         out_shape=[
             jax.ShapeDtypeStruct(block, bf),
-            jax.ShapeDtypeStruct(out.shape[1:], bf),
-            jax.ShapeDtypeStruct(weight.shape, bf),
+            jax.ShapeDtypeStruct(q.shape, bf),
+            jax.ShapeDtypeStruct(q.shape, bf),
+            jax.ShapeDtypeStruct(pieces, bf),
         ],
         scratch_shapes=[pltpu.VMEM(*shape) for shape in scratch] + sems,
         compiler_params=pltpu.CompilerParams(collective_id=1, has_side_effects=True),
         name="settle",
-    )(index, slots, dprior, down, out, weight)
+    )(index, q, da, prior, own, keys, seen, proj, cot)
 
 
 def on_device(
@@ -444,27 +450,18 @@
     seen = seen.astype(f32)[:, None]
 
     d_attended = jnp.dot(out_weight, cotangent_all, preferred_element_type=f32).astype(bf)
-    attended, d_queries, d_prior, d_own, d_slots = attend(
-        queries, d_attended, prior, own, slots.reshape(SLOTS * ROW_CELLS, width), seen
-    )
-    weight_part = lax.dot_general(
-        attended, cotangent_all, (((1,), (1,)), ((), ())), preferred_element_type=f32
-    )
-    high, wide = features // ROW_CELLS, weight_part.shape[1] // 128
-    pieces = weight_part.astype(bf).reshape(high, ROW_CELLS, wide, 128).transpose(0, 2, 1, 3)
-    pieces = pieces.reshape(NSIDE, LUMPS, ROW_CELLS, 128)
-    partial_out = lax.dot_general(
-        out_weight, attended, (((0,), (0,)), ((), ())), preferred_element_type=f32
-    )
-    block = (ROWS_BLK, ROW_CELLS, width)
-    total, mixed, weight_all = settle(
+    total, mixed, d_queries, weight_all = settle(
         index,
-        d_slots.reshape(NSIDE, NZ, ROW_CELLS, width),
-        d_prior.reshape(block),
-        d_own.reshape(block),
-        partial_out.astype(bf).reshape(nmp, features, CELLS_BLK),
-        pieces,
-    )
+        queries,
+        d_attended,
+        prior,
+        own,
+        slots.reshape(SLOTS * ROW_CELLS, width),
+        seen,
+        out_weight,
+        cotangent_all,
+    )
+    high, wide = features // ROW_CELLS, out_weight.shape[1] // 128
     weight_grad = weight_all.reshape(high, wide, ROW_CELLS, 128).transpose(0, 2, 1, 3)
     weight_grad = weight_grad.reshape(features, -1).astype(f32)
     d_pairs = total.reshape(CELLS_BLK, width).T.reshape(heads, 2, HEAD_DIM, CELLS_BLK)

time: 132 us -> 124 us (0.939)
  Pallas kernels: 113 us -> 107 us
    pallas_call x1 -> x0, Pallas kernels: 9.18 us -> none  [attend(): pl.pallas_call(attend_kernel, grid=(heads,), in_specs=[feat, feat, cells,...]
    pallas_call x1, Pallas kernels: 51.9 us -> 54.9 us  [settle(): pl.pallas_call(functools.partial(settle_kernel, nmp), in_specs=[pl.BlockS...]
where the time goes in v5:
time: 124 us; the launch traced here: 123 us
  Pallas kernels  107 us (86%)
  local copies, waits for them, and re-layouts  9.19 us (7%)
  other arithmetic  3.07 us (2%)
  between operations  2.01 us (2%)
  matrix products  1.86 us (2%)
    pallas_call x1, Pallas kernels, settle(): pl.pallas_call(functools.partial(settle_kernel, nmp), in_specs=[pl.BlockS...  54.9 us
    pallas_call x1, Pallas kernels, fetch(): pl.pallas_call(functools.partial(fetch_kernel, nmp, fanout), in_specs=[vm...  52.1 us

profile of v5, /device:TPU:1, one launch (start us, length us, event | category | flops | bytes accessed | tf_op | source)
XLA Modules:
  0.0 123.2 jit_solution(5236991756927887060)
XLA Ops:
  1.9 0.7 fusion.2
  2.6 0.7 pad_add_fusion
  3.3 0.1 multiply_add_fusion
  3.4 0.1 add.64
  3.5 0.1 compare_reduce_fusion
  3.6 0.6 broadcast_in_dim.7.info_ref
  4.2 0.1 broadcast_in_dim.16
  4.3 0.1 concatenate.26
  4.4 0.8 pad_maximum_fusion
  5.2 0.8 copy.34
  6.0 52.1 %fetch.1 = (bf16[8,16,16,384]{3,2,1,0:T(8,128)(2,1)}, s32[16,128]{1,0:T(8,128)}, bf16[4,192,128]{2,1,0:T(8,128)(2,1)}, bf16[8,16,384]{2,1,0:T(8,128)(2,1)}, s32[8,128]{1,0:T(8,128)}) custom-call(bf16[8,16,384]{2,1,0:T(8,128)(2,1)} %bitcast.40, s32[8,128]{1,0:T(8,128)} %broadcast_in_dim.7.info_ref, bf16[192,128]{1,0:T(8,128)(2,1)} %cot_ref.1), custom_call_target="tpu_custom_call" | custom-call | tf_op jit(solution)/shard_map/fetch/pallas_call | solution.py:198
  58.1 1.3 %slice.9 = s32[1,1]{1,0:T(1,128)} slice(s32[8,128]{1,0:T(8,128)} %get-tuple-element.18), slice={[0:1], [64:65]} | slice | bytes 8 | tf_op jit(solution)/shard_map/slice | solution.py:443
  59.3 0.7 compare_bitcast_fusion
  60.0 1.9 %fusion.da_ref = bf16[192,128]{1,0:T(8,128)(2,1)} fusion(bf16[192,768]{1,0:T(8,128)(2,1)} %proj_ref.1, bf16[768,128]{1,0:T(8,128)(2,1)} %bitcast.42), kind=kOutput, calls=%fused_computation.1 | convolution fusion | flops 37773312 | bytes 540672 | tf_op jit(solution)/shard_map/dot_general | solution.py:452
  61.9 1.4 %copy.35.seen_ref = f32[2304,1]{1,0:T(8,128)} copy(f32[2304,1]{0,1:T(1,128)S(1)} %add_convert_fusion) | data formatting | bytes 18432 | tf_op jit(solution)/shard_map/convert_element_type | solution.py:450
  63.3 54.9 %settle.1 = (bf16[8,16,384]{2,1,0:T(8,128)(2,1)}, bf16[192,128]{1,0:T(8,128)(2,1)}, bf16[192,128]{1,0:T(8,128)(2,1)}, bf16[8,9,16,128]{3,2,1,0:T(8,128)(2,1)}) custom-call(s32[16,128]{1,0:T(8,128)} %get-tuple-element.14.index_ref, bf16[192,128]{1,0:T(8,128)(2,1)} %q_ref.1, bf16[192,128]{1,0:T(8,128)(2,1)} %fusion.da_ref, bf16[128,384]{1,0:T(8,128)(2,1)} %bitcast.48, ...), custom_call_target="tpu_custom_call" | custom-call | tf_op jit(solution)/shard_map/settle/pallas_call | solution.py:404
  118.3 0.0 copy-start.1
  118.3 0.0 copy-start
  118.3 1.0 copy.36
  119.3 0.6 fusion.3
  120.0 1.0 copy.37
  121.0 0.9 copy.40
  121.9 0.0 copy-done.1
  121.9 0.6 copy.45
  122.5 0.0 copy-done
  122.6 0.6 copy.46
  (3 shorter events, 0.0 us)
Async XLA Ops:
  118.3 3.7 %copy-start.1 = (bf16[192,128]{1,0:T(8,128)(2,1)S(1)}, bf16[192,128]{1,0:T(8,128)(2,1)}, u32[]{:S(2)}) copy-start(bf16[192,128]{1,0:T(8,128)(2,1)} %get-tuple-element.34) | copy-start | bytes 147460
  118.3 4.3 %copy-start = (bf16[192,128]{1,0:T(8,128)(2,1)S(1)}, bf16[192,128]{1,0:T(8,128)(2,1)}, u32[]{:S(2)}) copy-start(bf16[192,128]{1,0:T(8,128)(2,1)} %get-tuple-element.35) | copy-start | bytes 147460
